TPU v7x, 32 devices: a whole 2x2x4 slice. The times are simulated.
32 devices in a mesh: orb: 8 (over y, x, core), grid: 4 (over z).
Axes of the slice: x: 2, y: 2, z: 4, core: 2. Of those that a mesh axis runs over, the one named last changes fastest.
Arguments:
- orbitals: float32 [128, 32, 4096], P('orb', 'grid'), may hold values from -6 to 6
- rotation: float32 [128, 128], replicated, may hold values from -0.5 to 0.5
- tile_list: int32 [4, 2], replicated, may hold values from 0 to 31, as said below
- pair_mask: int32 [128, 128], replicated, may hold values from 0 to 1, as said below
Outputs:
- exchange_term: float32 [128, 32, 4096], P('orb', 'grid')
Inputs may be any that keep to these rules, and one draw needn't show every extreme that they name: `tile_list`: row t names one tile: its target block and its source block of 4 orbitals each; no tile is named twice. `pair_mask`: among the 64 orbital pairs that lie in listed tiles, exactly 32 are 1.
All inputs are finite; a program needn't handle non-finite values.
Results may differ from a plain program's by a relative error of at most 0.0003.
Values sent between devices are 32-bit elements; how exact they have to be, the bound alone decides.
No kernel may reach another device: no remote copies, remote signals or barrier semaphores. Data moves between devices by JAX's collectives and lax.ppermute only.
A program may use at most 64 MiB of HBM per device.

v0:
```python
import jax
import jax.numpy as jnp
from jax import lax
from jax.sharding import PartitionSpec as P

NORB = 128
BLK = 4
NX = 32
NY = 64
NZ = 64
LIVE_DEV = 1


precise = lax.Precision.HIGHEST
coupling = 0.25
screening = 0.1


def sine_table(length):
    wave_index = jnp.arange(length, dtype=jnp.float32) + 1.0
    return jnp.sqrt(2.0 / (length + 1.0)) * jnp.sin(
        jnp.pi * wave_index[:, None] * wave_index[None, :] / (length + 1.0)
    )


def eigen_values(length):
    wave_index = jnp.arange(length, dtype=jnp.float32) + 1.0
    return 2.0 - 2.0 * jnp.cos(jnp.pi * wave_index / (length + 1.0))


def green_kernel(size_x, size_y, size_z):
    summed = (
        eigen_values(size_x)[:, None, None]
        + eigen_values(size_y)[None, :, None]
        + eigen_values(size_z)[None, None, :]
    )
    return coupling / (summed + screening)


def pair_lists(tile_list, pair_mask):
    within = jnp.arange(BLK * BLK, dtype=jnp.int32)
    targets = (BLK * tile_list[:, 0:1] + within[None, :] // BLK).reshape(-1)
    sources = (BLK * tile_list[:, 1:2] + within[None, :] % BLK).reshape(-1)
    return (targets, sources, pair_mask[targets, sources])


def compact(targets, sources, live_flags, number):
    ranking = jnp.cumsum(live_flags) - 1
    places = jnp.where(live_flags == 1, ranking, number)
    picked = (
        jnp.zeros((number,), jnp.int32)
        .at[places]
        .set(jnp.arange(live_flags.shape[0], dtype=jnp.int32), mode="drop")
    )
    return (targets[picked], sources[picked])


def along_z(values, matrix):
    number, planes, width_yz = values.shape
    size_z = matrix.shape[0]
    shaped = values.reshape(number, planes, width_yz // size_z, size_z)
    return jnp.einsum("pxrz,zk->pxrk", shaped, matrix, precision=precise).reshape(
        number, planes, width_yz
    )


def along_y(values, matrix):
    number, planes, width_yz = values.shape
    size_y = matrix.shape[0]
    shaped = values.reshape(number, planes, size_y, width_yz // size_y)
    return jnp.einsum("pxyz,yk->pxkz", shaped, matrix, precision=precise).reshape(
        number, planes, width_yz
    )


def along_x(values, matrix):
    return jnp.einsum("pxc,xk->pkc", values, matrix, precision=precise)


def on_device(orbitals, rotation, tile_list, pair_mask):
    rotated = jnp.einsum(
        "ij,ixc->jxc",
        rotation,
        lax.all_to_all(orbitals, "orb", split_axis=2, concat_axis=0, tiled=True),
        precision=precise,
    )
    planes = rotated.shape[1]
    width_yz = rotated.shape[2]
    targets, sources, live_flags = pair_lists(tile_list, pair_mask)
    matrix_x = sine_table(NX)
    matrix_y = sine_table(NY)
    matrix_z = sine_table(NZ)
    kernel = green_kernel(NX, NY, NZ).reshape(NX, NY * NZ)
    orbital_ids = jnp.arange(NORB, dtype=jnp.int32)
    targets, sources = compact(
        targets, sources, live_flags, LIVE_DEV * lax.axis_size("orb") * lax.axis_size("grid")
    )
    density = rotated[targets] * rotated[sources]
    number = density.shape[0]
    spectrum = along_z(density, matrix_z)
    spectrum = lax.all_to_all(spectrum, "orb", split_axis=0, concat_axis=2, tiled=True)
    spectrum = along_y(spectrum, matrix_y)
    spectrum = lax.all_to_all(spectrum, "grid", split_axis=0, concat_axis=1, tiled=True)
    spectrum = along_x(along_x(spectrum, matrix_x) * kernel, matrix_x)
    spectrum = lax.all_to_all(spectrum, "grid", split_axis=1, concat_axis=0, tiled=True)
    spectrum = along_y(spectrum, matrix_y)
    spectrum = lax.all_to_all(spectrum, "orb", split_axis=2, concat_axis=0, tiled=True)
    potential = along_z(spectrum, matrix_z)
    products = potential * rotated[sources]
    selector = (targets[None, :] == orbital_ids[:, None]).astype(jnp.float32)
    partial_value = -jnp.dot(
        selector, products.reshape(number, planes * width_yz), precision=precise
    )
    partial_value = partial_value.reshape(NORB, planes, width_yz)
    return lax.all_to_all(partial_value, "orb", split_axis=0, concat_axis=2, tiled=True)


def solution(mesh):
    in_specs = (P("orb", "grid", None), P(), P(), P())
    out_specs = P("orb", "grid", None)
    return jax.shard_map(
        on_device, mesh=mesh, in_specs=in_specs, out_specs=out_specs, check_vma=False
    )
```

profile of v0, /device:TPU:0, one launch (start us, length us, event | category | flops | bytes accessed | tf_op | source)
XLA Modules:
  0.0 235.5 jit_solution(4577245099741544365)
XLA Ops:
  0.0 9.6 %copy.93 = f32[16,8,4096]{0,1,2:T(8,128)} copy(f32[16,8,4096]{2,1,0:T(8,128)} %param.4) | data formatting | bytes 4194304 | tf_op args[0]
  9.6 11.6 %reshape.364 = f32[8,1,65536]{2,1,0:T(1,128)} reshape(f32[4096,8,16]{2,1,0:T(8,128)} %bitcast.76) | data formatting | bytes 4194304
  21.2 5.3 %all-to-all-start = ((f32[8,1,65536]{2,1,0:T(1,128)}), f32[8,1,65536]{2,1,0:T(1,128)S(1)}, u32[]{:S(2)}, u32[]{:S(2)}) async-start(f32[8,1,65536]{2,1,0:T(1,128)} %reshape.364), calls=%async_computation | async-start | bytes 4194304 | tf_op jit(solution)/shard_map/all_to_all | solution.py:84
  27.1 0.8 gather_fusion
  28.2 0.9 scatter_custom_fusion
  29.2 0.7 gather_fusion.1
  29.9 0.7 gather_fusion.3
  30.7 22.5 %all-to-all-done = f32[8,1,65536]{2,1,0:T(1,128)S(1)} async-done(((f32[8,1,65536]{2,1,0:T(1,128)}), f32[8,1,65536]{2,1,0:T(1,128)S(1)}, u32[]{:S(2)}, u32[]{:S(2)}) %all-to-all-start) | async-done | bytes 2097184 | tf_op jit(solution)/shard_map/all_to_all | solution.py:84
  53.1 1.3 copy-done.2
  54.4 0.5 broadcast.433
  55.0 7.1 %reduce.5 = f32[8,65536]{1,0:T(8,128)S(1)} reduce(f32[8,1,65536]{2,1,0:T(1,128)} %copy-done.2, f32[]{:T(128)} %broadcast.433), dimensions={1}, to_apply=%all_to_all.62.reduce_sub_computation | reduce | bytes 4194308 | tf_op jit(solution)/shard_map/all_to_all | solution.py:84
  62.1 11.2 %reshape.365 = f32[4096,8,16]{2,1,0:T(8,128)} reshape(f32[8,65536]{1,0:T(8,128)S(1)} %reduce.5) | data formatting | bytes 4194304
  73.3 10.0 %copy.94 = f32[16,8,8,512]{3,0,2,1:T(8,128)S(1)} copy(f32[16,8,8,512]{0,1,3,2:T(8,128)} %bitcast.75) | data formatting | bytes 4194304 | tf_op jit(solution)/shard_map/all_to_all | solution.py:84
  83.3 1.9 fusion.6
  85.2 1.2 copy.96
  86.5 0.6 gather_fusion.2
  87.1 0.6 gather_fusion.4
  87.9 1.8 fusion.2
  89.7 0.6 copy.99
  90.6 12.1 %all_to_all.84 = f32[32,8,512]{2,1,0:T(8,128)S(1)} all-to-all(f32[32,8,512]{2,1,0:T(8,128)S(1)} %reshape.298), channel_id=1, replica_groups=mesh['orb'=8,'grid'=4] {'orb'}, dimensions={0} | all-to-all | bytes 1048576 | tf_op jit(solution)/shard_map/all_to_all | solution.py:101
  103.3 1.2 convolution_bitcast_fusion.2
  104.5 1.2 reshape.300
  105.6 4.9 %all-to-all-start.2 = ((f32[4,8,4096]{2,1,0:T(8,128)}), f32[4,8,4096]{2,1,0:T(8,128)S(1)}, u32[]{:S(2)}, u32[]{:S(2)}) async-start(f32[4,8,4096]{2,1,0:T(8,128)} %reshape.300), calls=%async_computation.2 | async-start | bytes 1048576 | tf_op jit(solution)/shard_map/all_to_all | solution.py:103
  110.7 0.3 add.258
  111.0 0.4 add.259
  111.5 13.0 %all-to-all-done.2 = f32[4,8,4096]{2,1,0:T(8,128)S(1)} async-done(((f32[4,8,4096]{2,1,0:T(8,128)}), f32[4,8,4096]{2,1,0:T(8,128)S(1)}, u32[]{:S(2)}, u32[]{:S(2)}) %all-to-all-start.2) | async-done | bytes 524320 | tf_op jit(solution)/shard_map/all_to_all | solution.py:103
  124.4 0.8 convolution_multiply_fusion
  125.2 0.8 convolution_bitcast_fusion
  126.0 0.5 copy.102
  126.5 16.9 %all_to_all.85 = f32[1,32,4096]{2,0,1:T(1,128)S(1)} all-to-all(f32[1,32,4096]{2,0,1:T(1,128)S(1)} %copy.102), channel_id=1, replica_groups=mesh['orb'=8,'grid'=4] {'grid'}, dimensions={1} | all-to-all | bytes 1048576 | tf_op jit(solution)/shard_map/all_to_all | solution.py:105
  143.4 1.2 reduce.2
  144.7 0.4 reshape.302
  145.1 1.2 convolution_bitcast_fusion.1
  146.3 5.9 %copy.117 = f32[4,8,64,64]{1,0,3,2:T(4,128)} copy(f32[4,8,64,64]{3,2,1,0:T(8,128)S(1)} %convolution_bitcast_fusion.1) | data formatting | bytes 1048576 | tf_op jit(solution)/shard_map/reshape | solution.py:71
  152.2 12.1 %reshape.366 = f32[8,1,16384]{2,1,0:T(1,128)} reshape(f32[4096,4,8]{2,1,0:T(4,128)} %bitcast.77) | data formatting | bytes 1048576
  164.3 3.5 %all-to-all-start.4 = ((f32[8,1,16384]{2,1,0:T(1,128)}), f32[8,1,16384]{2,1,0:T(1,128)S(1)}, u32[]{:S(2)}, u32[]{:S(2)}) async-start(f32[8,1,16384]{2,1,0:T(1,128)} %reshape.366), calls=%async_computation.4 | async-start | bytes 1048576 | tf_op jit(solution)/shard_map/all_to_all | solution.py:107
  167.8 0.3 copy.120
  168.1 9.3 %all-to-all-done.4 = f32[8,1,16384]{2,1,0:T(1,128)S(1)} async-done(((f32[8,1,16384]{2,1,0:T(1,128)}), f32[8,1,16384]{2,1,0:T(1,128)S(1)}, u32[]{:S(2)}, u32[]{:S(2)}) %all-to-all-start.4) | async-done | bytes 524320 | tf_op jit(solution)/shard_map/all_to_all | solution.py:107
  177.5 1.8 reduce.6
  179.3 13.1 %reshape.367 = f32[4096,4,8]{2,1,0:T(4,128)} reshape(f32[8,16384]{1,0:T(8,128)S(1)} %reduce.6) | data formatting | bytes 1048576
  192.4 6.8 %copy.119 = f32[4,8,8,512]{3,1,0,2:T(8,128)S(1)} copy(f32[4,8,8,512]{1,0,3,2:T(4,128)} %bitcast.78) | data formatting | bytes 1048576 | tf_op jit(solution)/shard_map/all_to_all | solution.py:107
  199.4 1.8 fusion
  201.2 0.6 copy.108
  201.8 0.4 reshape.305
  202.2 1.0 convolution_negate_fusion
  203.2 1.6 copy.121
  204.8 29.0 %all_to_all.86 = f32[128,8,512]{2,1,0:T(8,128)S(1)} all-to-all(f32[128,8,512]{2,1,0:T(8,128)S(1)} %bitcast.81), channel_id=1, replica_groups=mesh['orb'=8,'grid'=4] {'orb'}, dimensions={0} | all-to-all | bytes 4194304 | tf_op jit(solution)/shard_map/all_to_all | solution.py:115
  233.8 1.5 copy.109
  (41 shorter events, 2.4 us)
Async XLA Ops:
  0.0 83.3 %copy-start = (f32[128,128]{1,0:T(8,128)S(1)}, f32[128,128]{1,0:T(8,128)}, u32[]{:S(2)}) copy-start(f32[128,128]{1,0:T(8,128)} %param.5) | copy-start | bytes 196612
  21.2 5.4 %copy-start.4 = (s32[4,2]{0,1:T(2,128)S(1)}, s32[4,2]{0,1:T(2,128)}, u32[]{:S(2)}) copy-start(s32[4,2]{0,1:T(2,128)} %param.6) | copy-start | bytes 100
  21.2 5.9 %copy-start.3 = (s32[128,128]{1,0:T(8,128)S(1)}, s32[128,128]{1,0:T(8,128)}, u32[]{:S(2)}) copy-start(s32[128,128]{1,0:T(8,128)} %param.7) | copy-start | bytes 196612
  21.2 31.9 %all-to-all-start = ((f32[8,1,65536]{2,1,0:T(1,128)}), f32[8,1,65536]{2,1,0:T(1,128)S(1)}, u32[]{:S(2)}, u32[]{:S(2)}) async-start(f32[8,1,65536]{2,1,0:T(1,128)} %reshape.364), calls=%async_computation | async-start | bytes 4194304 | tf_op jit(solution)/shard_map/all_to_all | solution.py:84
  53.1 1.3 copy-start.2
  105.6 18.8 %all-to-all-start.2 = ((f32[4,8,4096]{2,1,0:T(8,128)}), f32[4,8,4096]{2,1,0:T(8,128)S(1)}, u32[]{:S(2)}, u32[]{:S(2)}) async-start(f32[4,8,4096]{2,1,0:T(8,128)} %reshape.300), calls=%async_computation.2 | async-start | bytes 1048576 | tf_op jit(solution)/shard_map/all_to_all | solution.py:103
  164.3 13.2 %all-to-all-start.4 = ((f32[8,1,16384]{2,1,0:T(1,128)}), f32[8,1,16384]{2,1,0:T(1,128)S(1)}, u32[]{:S(2)}, u32[]{:S(2)}) async-start(f32[8,1,16384]{2,1,0:T(1,128)} %reshape.366), calls=%async_computation.4 | async-start | bytes 1048576 | tf_op jit(solution)/shard_map/all_to_all | solution.py:107
  233.8 1.5 copy-start.1
where the time goes:
time: 239 us; the launch traced here: 236 us
  local copies, waits for them, and re-layouts  97.2 us (41%)
  blocking collectives  58 us (24%)
  waiting for transfers between devices  44.8 us (19%)
  starting transfers between devices  13.7 us (6%)
  other arithmetic  10.9 us (5%)
  matrix products  10.4 us (4%)
    unnamed x17, local copies, waits for them, and re-layouts  60.9 us
    all_to_all x1, blocking collectives, on_device(): lax.all_to_all(partial_value, 'orb', split_axis=0, concat_axis=2, tiled=T...  29 us
    all_to_all x1, waiting for transfers between devices, on_device(): lax.all_to_all(orbitals, 'orb', split_axis=2, concat_axis=0, tiled=True)  22.5 us
    all_to_all x1, blocking collectives, on_device(): lax.all_to_all(spectrum, 'grid', split_axis=1, concat_axis=0, tiled=True)  16.9 us
    all_to_all x1, waiting for transfers between devices, on_device(): lax.all_to_all(spectrum, 'grid', split_axis=0, concat_axis=1, tiled=True)  13 us
    all_to_all x1, blocking collectives, on_device(): lax.all_to_all(spectrum, 'orb', split_axis=0, concat_axis=2, tiled=True)  12.1 us
    all_to_all x2, local copies, waits for them, and re-layouts, on_device(): lax.all_to_all(orbitals, 'orb', split_axis=2, concat_axis=0, tiled=True)  10.5 us
    all_to_all x1, waiting for transfers between devices, on_device(): lax.all_to_all(spectrum, 'orb', split_axis=2, concat_axis=0, tiled=True)  9.33 us
  transfers between devices with their start and end apart: 3, of which 3 were waited for; matrix products, arithmetic and copies ran while one was open for 2% of the time, Pallas kernels for 0%

commit v1 on v0

v1 whole, which is shorter than its diff:
```python
import functools

import jax
import jax.numpy as jnp
import numpy as np
from jax import lax
from jax.experimental import pallas as pl
from jax.experimental.pallas import tpu as pltpu
from jax.sharding import PartitionSpec as P

BLK = 4
NY = 64
NZ = 64
LANES = 128
SUB = 8
COUPLING = 0.25
SCREENING = 0.1

precise = lax.Precision.HIGHEST
f32 = jnp.float32
bf16 = jnp.bfloat16


def sine_np(n):
    k = np.arange(1, n + 1, dtype=np.float64)
    return np.sqrt(2.0 / (n + 1)) * np.sin(np.pi * k[:, None] * k[None, :] / (n + 1))


def eigen_np(n):
    k = np.arange(1, n + 1, dtype=np.float64)
    return 2.0 - 2.0 * np.cos(np.pi * k / (n + 1))


def halves_np(table):
    high = np.asarray(table, np.float32).astype(jnp.bfloat16)
    low = (np.asarray(table, np.float64) - high.astype(np.float64)).astype(jnp.bfloat16)
    return jnp.asarray(high), jnp.asarray(low)


def y_order():
    rows = LANES // NZ
    return np.arange(NY).reshape(NY // rows, rows).T.reshape(-1)


def y_table():
    order = y_order()
    return np.kron(sine_np(NY)[order][:, order], np.eye(SUB))


def z_table():
    half = LANES // NZ
    sine = sine_np(NZ)
    table = np.zeros((2, half, NZ, half, 2, NZ))
    for pair in range(2):
        for h in range(half):
            table[pair, h, :, h, pair, :] = sine
    return table.reshape(2 * half * NZ, half * 2 * NZ)


def decay_np():
    c = eigen_np(NY)[y_order()][:, None] + eigen_np(NZ)[None, :] + SCREENING
    r = 2.0 / (2.0 + c + np.sqrt(c * (c + 4.0)))
    return np.concatenate([r, r], axis=1)


def dot(a, b):
    return jnp.dot(a, b, preferred_element_type=f32)


def split(x):
    high = x.astype(bf16)
    return high, (x - high.astype(f32)).astype(bf16)


def dot3(a, b):
    return dot(a[0], b[0]) + dot(a[0], b[1]) + dot(a[1], b[0])


def rotate_kernel(own, sib, mine, theirs, send, keep):
    rows, width = send.shape[0] * SUB, send.shape[2]
    depth = mine.shape[0] * SUB
    a = split(mine[...].reshape(depth, width))
    b = split(theirs[...].reshape(depth, width))
    for out, at in ((send, 0), (keep, rows)):
        part = pl.ds(at, rows)
        total = dot3(split(own[part, :]), a) + dot3(split(sib[part, :]), b)
        out[...] = total.reshape(out.shape)


def forward_kernel(u, where, own, other, y_hi, y_lo, z_hi, z_lo, decay, left, right, k_left, k_right,
                   local, a_out, b_out, dens, work, fwd, bwd):
    tiles = own.shape[2] // LANES
    core = where[0]
    for side, ref, source, target in ((0, own, BLK // 2, BLK // 2 + BLK + u), (1, other, 2, u)):
        offset = jnp.where(core == side, 0, tiles * SUB) if side == 0 else jnp.where(core == 0, tiles * SUB, 0)
        for t in range(tiles):
            lanes = pl.ds(t * LANES, LANES)
            value = ref[target, :, lanes]
            rows = pl.ds(pl.multiple_of(offset + t * SUB, SUB), SUB)
            for w in range(BLK):
                dens[rows, w * LANES:(w + 1) * LANES] = value * ref[source + w, :, lanes]
    z = (z_hi[...], z_lo[...])
    half = dens.shape[0]
    for q in range(BLK // 2):
        out = dot3(split(dens[:, q * 2 * LANES:(q + 1) * 2 * LANES]), z)
        work[:half, q * LANES:(q + 1) * LANES] = out[:, :LANES]
        work[half:, q * LANES:(q + 1) * LANES] = out[:, LANES:]
    work[...] = dot3((y_hi[...], y_lo[...]), split(work[...]))
    plane = lax.broadcasted_iota(jnp.int32, (SUB, LANES), 0)

    def solve(k, carry):
        rows = pl.ds(pl.multiple_of(k * SUB, SUB), SUB)
        r = decay[rows, :]
        steps = []
        power = r
        for s in (1, 2, 4):
            steps.append((s, jnp.where(plane >= s, power, 0.0), jnp.where(plane < SUB - s, power, 0.0)))
            power = power * power
        lf, rt, kl, kr = left[rows, :], right[rows, :], k_left[rows, :], k_right[rows, :]
        for q in range(BLK // 2):
            lanes = slice(q * LANES, (q + 1) * LANES)
            rho = work[rows, lanes]
            f = lf * rho
            own_term = rt * rho
            h = own_term
            for s, down, up in steps:
                f = f + down * pltpu.roll(f, s, 0)
                h = h + up * pltpu.roll(h, SUB - s, 0)
            fwd[q, rows, :] = f
            bwd[q, rows, :] = h
            local[rows, lanes] = kl * f + kr * (h - own_term)
        return carry

    lax.fori_loop(0, NY, solve, 0, unroll=4)
    for q in range(BLK // 2):
        lanes = slice(q * LANES, (q + 1) * LANES)
        a_out[:, lanes] = fwd[q, pl.ds(SUB - 1, NY, stride=SUB), :]
        b_out[:, lanes] = bwd[q, pl.ds(0, NY, stride=SUB), :]


def backward_kernel(u, where, flags, own, other, y_hi, y_lo, z_hi, z_lo, local, from_left, from_right,
                    in_left, in_right, out, work, pot):
    tiles = own.shape[2] // LANES
    core = where[0]

    def add(group, carry):
        lines = pl.ds(pl.multiple_of(group * SUB, SUB), SUB)
        for q in range(BLK // 2):
            lanes = slice(q * LANES, (q + 1) * LANES)
            lp, rp = from_left[lines, lanes], from_right[lines, lanes]
            for k in range(SUB):
                rows = pl.ds(pl.multiple_of((group * SUB + k) * SUB, SUB), SUB)
                here = in_left[rows, :] * lp[k:k + 1] + in_right[rows, :] * rp[k:k + 1]
                work[rows, lanes] = local[rows, lanes] + here
        return carry

    lax.fori_loop(0, NY // SUB, add, 0)
    work[...] = dot3((y_hi[...], y_lo[...]), split(work[...]))
    z = (z_hi[...], z_lo[...])
    half = pot.shape[0]
    for q in range(BLK // 2):
        lanes = slice(q * LANES, (q + 1) * LANES)
        rows = jnp.concatenate([work[:half, lanes], work[half:, lanes]], axis=1)
        pot[:, q * 2 * LANES:(q + 1) * 2 * LANES] = dot3(split(rows), z)
    for side, ref, source in ((0, own, BLK // 2), (1, other, 2)):
        offset = jnp.where(core == 0, 0, tiles) if side == 0 else jnp.where(core == 0, tiles, 0)
        for t in range(tiles):
            lanes = pl.ds(t * LANES, LANES)
            rows = pl.ds(pl.multiple_of((offset + t) * SUB, SUB), SUB)
            total = None
            for w in range(BLK):
                term = flags[u * BLK + w] * (pot[rows, w * LANES:(w + 1) * LANES] * ref[source + w, :, lanes])
                total = term if total is None else total + term
            out[:, pl.ds(pl.multiple_of((offset + t) * LANES, LANES), LANES)] = -total


def place_kernel(match, *refs):
    parts, out = refs[:-1], refs[-1]
    blocks = out.shape[0] // BLK
    count = len(parts) // 2
    for b in range(blocks):
        for own_core in range(2):
            for u in range(BLK // 2):
                total = None
                for n in range(count):
                    ref = parts[own_core * count + n]
                    term = match[(b * 2 + own_core) * count + n] * ref[u]
                    total = term if total is None else total + term
                row = match_row(out, b, u, own_core)
                out[row] = total


def match_row(out, b, u, own_core):
    core = lax.rem(lax.axis_index("orb"), 2)
    which = core if own_core == 0 else 1 - core
    return b * BLK + which * (BLK // 2) + u


VM = pl.BlockSpec(memory_space=pltpu.VMEM)
SM = pl.BlockSpec(memory_space=pltpu.SMEM)


def tile_device(orbitals, rotation, tile_list, pair_mask):
    per_device, planes, width = orbitals.shape
    n_orb, n_grid = lax.axis_size("orb"), lax.axis_size("grid")
    size_x = planes * n_grid
    half = width // 2
    axes = ("orb", "grid")
    o, g = lax.axis_index("orb"), lax.axis_index("grid")
    core, chip = o % 2, o // 2

    def swap(x, even, odd):
        moves = []
        for a in range(n_orb):
            flip = even if a % 2 == 0 else odd
            moves += [(a * n_grid + b, (a ^ flip) * n_grid + b) for b in range(n_grid)]
        return lax.ppermute(x, axes, moves)

    def shift(x, step):
        moves = [(a * n_grid + b, a * n_grid + b + step) for a in range(n_orb)
                 for b in range(n_grid) if 0 <= b + step < n_grid]
        return lax.ppermute(x, axes, moves)

    low, high = orbitals[:, :, :half], orbitals[:, :, half:]
    mine = jnp.where(core == 0, low, high)
    theirs = swap(jnp.where(core == 0, high, low), 1, 1)

    bit_1 = jnp.where(core == 0, 1, 2)
    bit_2 = 3 - bit_1
    order = jnp.stack([chip ^ 3, chip ^ bit_1, chip ^ bit_2, chip])
    blocks = tile_list[order]
    pick = jnp.arange(BLK // 2)
    wanted = jnp.concatenate(
        [
            BLK * blocks[:, 0:1] + (BLK // 2) * (1 - core) + pick,
            BLK * blocks[:, 1:2] + jnp.arange(BLK),
            BLK * blocks[:, 0:1] + (BLK // 2) * core + pick,
        ],
        axis=1,
    ).reshape(-1)
    chosen = (jnp.repeat(wanted, SUB)[:, None] == jnp.arange(rotation.shape[1])[None, :]).astype(f32)
    rows = jnp.einsum("rj,ij->ri", chosen, rotation, precision=precise)
    same_plane = jnp.arange(chosen.shape[0])[:, None] % SUB == jnp.arange(per_device * SUB)[None, :] % SUB

    def spread(who):
        source = who * per_device + jnp.arange(per_device * SUB) // SUB
        columns = (jnp.arange(rotation.shape[0])[:, None] == source[None, :]).astype(f32)
        table = jnp.einsum("ri,ic->rc", rows, columns, precision=precise)
        return jnp.where(same_plane, table, 0.0)

    slots = wanted.shape[0]
    part = jax.ShapeDtypeStruct((slots // 2, planes, half), f32)
    send, keep = pl.pallas_call(
        rotate_kernel, out_shape=(part, part), in_specs=[VM] * 4, out_specs=(VM, VM), name="rotate",
    )(spread(o), spread(o ^ 1), mine, theirs)
    keep = keep + swap(send, 2, 4)
    cut = slots // 4
    own = keep[cut:] + swap(keep[:cut], 4, 2)
    other = swap(own[: cut - BLK // 2], 1, 1)

    decay = decay_np()
    log_r = jnp.asarray(np.log(decay), f32)[:, None, :]
    p = jnp.arange(planes, dtype=f32)[None, :, None]
    place = planes * g.astype(f32) + p + 1.0
    left = 1.0 - jnp.exp(2.0 * place * log_r)
    right = 1.0 - jnp.exp(2.0 * (size_x + 1.0 - place) * log_r)
    scale = jnp.asarray(COUPLING * decay / ((1 - decay**2) * (1 - decay ** (2 * size_x + 2))), f32)[:, None, :]
    k_left, k_right = scale * right, scale * left
    in_left = (k_left * jnp.exp((p + 1.0) * log_r)).reshape(-1, LANES)
    in_right = (k_right * jnp.exp((planes - p) * log_r)).reshape(-1, LANES)
    left, right, k_left, k_right = (v.reshape(-1, LANES) for v in (left, right, k_left, k_right))
    spread_decay = jnp.asarray(np.repeat(decay, SUB, axis=0), f32)
    slab = np.concatenate([decay, decay], axis=1) ** planes

    y_hi, y_lo = halves_np(y_table())
    z_hi, z_lo = halves_np(z_table())
    zt_hi, zt_lo = halves_np(z_table().T)
    where = jnp.stack([core, g]).astype(jnp.int32)
    tile = tile_list[chip]
    flags = lax.dynamic_slice(
        pair_mask, (BLK * tile[0] + (BLK // 2) * core, BLK * tile[1]), (BLK // 2, BLK)
    ).astype(f32).reshape(-1)

    solved = []
    for u in range(BLK // 2):
        lines = jax.ShapeDtypeStruct((NY, 2 * LANES), f32)
        cube = (NY * SUB, 2 * LANES)
        local, a, b = pl.pallas_call(
            functools.partial(forward_kernel, u),
            out_shape=(jax.ShapeDtypeStruct(cube, f32), lines, lines),
            in_specs=[SM] + [VM] * 11,
            out_specs=(VM, VM, VM),
            scratch_shapes=[pltpu.VMEM((width // LANES * SUB, BLK * LANES), f32), pltpu.VMEM(cube, f32)]
            + [pltpu.VMEM((BLK // 2, NY * SUB, LANES), f32)] * 2,
            name=f"forward_{u}",
        )(where, own, other, y_hi, y_lo, z_hi, z_lo, spread_decay, left, right, k_left, k_right)
        from_left = from_right = None
        step = 1
        while step < n_grid:
            got_a, got_b = shift(a, step), shift(b, -step)
            if from_left is None:
                from_left, from_right = got_a, got_b
            else:
                factor = jnp.asarray(slab ** (step - 1), f32)
                from_left, from_right = from_left + factor * got_a, from_right + factor * got_b
            factor = jnp.asarray(slab**step, f32)
            a, b = a + factor * got_a, b + factor * got_b
            step *= 2
        solved.append((local, from_left, from_right))

    terms = []
    for u, (local, from_left, from_right) in enumerate(solved):
        terms.append(pl.pallas_call(
            functools.partial(backward_kernel, u),
            out_shape=jax.ShapeDtypeStruct((planes, width), f32),
            in_specs=[SM, SM] + [VM] * 11,
            out_specs=VM,
            scratch_shapes=[pltpu.VMEM(cube, f32), pltpu.VMEM((width // LANES * SUB, BLK * LANES), f32)],
            name=f"backward_{u}",
        )(where, flags, own, other, y_hi, y_lo, zt_hi, zt_lo, local, from_left, from_right, in_left, in_right))

    term = jnp.stack(terms)
    near_1 = swap(term, 2, 4)
    near_2 = swap(term, 4, 2)
    far = swap(near_1, 4, 2)
    own_parts = [term, near_1, near_2, far]
    sib_parts = [swap(v, 1, 1) for v in own_parts]
    own_tiles = jnp.stack([chip, chip ^ bit_1, chip ^ bit_2, chip ^ 3])
    sib_tiles = jnp.stack([chip, chip ^ bit_2, chip ^ bit_1, chip ^ 3])
    home = tile_list[:, 0][jnp.stack([own_tiles, sib_tiles])]
    base = o * (per_device // BLK) + jnp.arange(per_device // BLK)
    match = (base[:, None, None] == home[None]).astype(f32).reshape(-1)
    chunk = width // 4
    spec = pl.BlockSpec((BLK // 2, planes, chunk), lambda i: (0, 0, i))
    return pl.pallas_call(
        place_kernel,
        out_shape=jax.ShapeDtypeStruct(orbitals.shape, f32),
        grid=(width // chunk,),
        in_specs=[SM] + [spec] * 8,
        out_specs=pl.BlockSpec((per_device, planes, chunk), lambda i: (0, 0, i)),
        name="place",
    )(match, *own_parts, *sib_parts)


def sine_table(length):
    wave_index = jnp.arange(length, dtype=f32) + 1.0
    return jnp.sqrt(2.0 / (length + 1.0)) * jnp.sin(
        jnp.pi * wave_index[:, None] * wave_index[None, :] / (length + 1.0)
    )


def eigen_values(length):
    wave_index = jnp.arange(length, dtype=f32) + 1.0
    return 2.0 - 2.0 * jnp.cos(jnp.pi * wave_index / (length + 1.0))


def green_kernel(size_x, size_y, size_z):
    summed = (
        eigen_values(size_x)[:, None, None]
        + eigen_values(size_y)[None, :, None]
        + eigen_values(size_z)[None, None, :]
    )
    return COUPLING / (summed + SCREENING)


def pair_lists(tile_list, pair_mask):
    within = jnp.arange(BLK * BLK, dtype=jnp.int32)
    targets = (BLK * tile_list[:, 0:1] + within[None, :] // BLK).reshape(-1)
    sources = (BLK * tile_list[:, 1:2] + within[None, :] % BLK).reshape(-1)
    return (targets, sources, pair_mask[targets, sources])


def compact(targets, sources, live_flags, number):
    ranking = jnp.cumsum(live_flags) - 1
    places = jnp.where(live_flags == 1, ranking, number)
    picked = (
        jnp.zeros((number,), jnp.int32)
        .at[places]
        .set(jnp.arange(live_flags.shape[0], dtype=jnp.int32), mode="drop")
    )
    return (targets[picked], sources[picked])


def along_z(values, matrix):
    number, planes, width_yz = values.shape
    size_z = matrix.shape[0]
    shaped = values.reshape(number, planes, width_yz // size_z, size_z)
    return jnp.einsum("pxrz,zk->pxrk", shaped, matrix, precision=precise).reshape(number, planes, width_yz)


def along_y(values, matrix):
    number, planes, width_yz = values.shape
    size_y = matrix.shape[0]
    shaped = values.reshape(number, planes, size_y, width_yz // size_y)
    return jnp.einsum("pxyz,yk->pxkz", shaped, matrix, precision=precise).reshape(number, planes, width_yz)


def along_x(values, matrix):
    return jnp.einsum("pxc,xk->pkc", values, matrix, precision=precise)


def any_device(orbitals, rotation, tile_list, pair_mask):
    n_orb, n_grid = lax.axis_size("orb"), lax.axis_size("grid")
    number_orbitals, size_x = rotation.shape[0], orbitals.shape[1] * n_grid
    rotated = jnp.einsum(
        "ij,ixc->jxc",
        rotation,
        lax.all_to_all(orbitals, "orb", split_axis=2, concat_axis=0, tiled=True),
        precision=precise,
    )
    planes, width_yz = rotated.shape[1:]
    targets, sources, live_flags = pair_lists(tile_list, pair_mask)
    matrix_x, matrix_y, matrix_z = sine_table(size_x), sine_table(NY), sine_table(NZ)
    kernel = green_kernel(size_x, NY, NZ).reshape(size_x, NY * NZ)
    orbital_ids = jnp.arange(number_orbitals, dtype=jnp.int32)
    targets, sources = compact(targets, sources, live_flags, targets.shape[0] // 2)
    density = rotated[targets] * rotated[sources]
    number = density.shape[0]
    spectrum = along_z(density, matrix_z)
    spectrum = lax.all_to_all(spectrum, "orb", split_axis=0, concat_axis=2, tiled=True)
    spectrum = along_y(spectrum, matrix_y)
    spectrum = lax.all_to_all(spectrum, "grid", split_axis=0, concat_axis=1, tiled=True)
    spectrum = along_x(along_x(spectrum, matrix_x) * kernel, matrix_x)
    spectrum = lax.all_to_all(spectrum, "grid", split_axis=1, concat_axis=0, tiled=True)
    spectrum = along_y(spectrum, matrix_y)
    spectrum = lax.all_to_all(spectrum, "orb", split_axis=2, concat_axis=0, tiled=True)
    potential = along_z(spectrum, matrix_z)
    products = potential * rotated[sources]
    selector = (targets[None, :] == orbital_ids[:, None]).astype(f32)
    partial_value = -jnp.dot(selector, products.reshape(number, planes * width_yz), precision=precise)
    partial_value = partial_value.reshape(number_orbitals, planes, width_yz)
    return lax.all_to_all(partial_value, "orb", split_axis=0, concat_axis=2, tiled=True)


def solution(mesh):
    n_orb, n_grid = mesh.shape["orb"], mesh.shape["grid"]

    def on_device(orbitals, rotation, tile_list, pair_mask):
        per_device, planes, width = orbitals.shape
        fits = n_orb == 8 and 2 * tile_list.shape[0] == n_orb and planes == SUB and per_device % BLK == 0
        fits = fits and width == NY * NZ and 2 * NZ == LANES
        body = tile_device if fits else any_device
        return body(orbitals, rotation, tile_list, pair_mask)

    in_specs = (P("orb", "grid", None), P(), P(), P())
    out_specs = P("orb", "grid", None)
    return jax.shard_map(on_device, mesh=mesh, in_specs=in_specs, out_specs=out_specs, check_vma=False)
```

time: 239 us -> 116 us (0.49)
  local copies, waits for them, and re-layouts: 97.2 us -> 7.55 us
  blocking collectives: 58 us -> 0 us
  Pallas kernels: 0 us -> 25.4 us
  starting transfers between devices: 13.7 us -> 30.8 us
  matrix products: 10.4 us -> 1.99 us
  waiting for transfers between devices: 44.8 us -> 37 us
    all_to_all x3 -> x0, blocking collectives: 58 us -> none  [the longest x1 29 us: on_device(): lax.all_to_all(partial_value, 'orb', split_axis=0, concat_axis=2, tiled=T...]
    unnamed x17 -> x39, local copies, waits for them, and re-layouts: 60.9 us -> 3.37 us
    all_to_all x3 -> x0, waiting for transfers between devices: 44.8 us -> none  [the longest x1 22.5 us: on_device(): lax.all_to_all(orbitals, 'orb', split_axis=2, concat_axis=0, tiled=True)]
    ppermute x0 -> x19, waiting for transfers between devices: none -> 37 us  [the longest x11 29.5 us: swap(): return lax.ppermute(x, axes, moves)]
    ppermute x0 -> x19, starting transfers between devices: none -> 30.8 us  [the longest x8 20.6 us: shift(): return lax.ppermute(x, axes, moves)]
    pallas_call x0 -> x6, Pallas kernels: none -> 25.4 us  [the longest x2 8.73 us: tile_device(): pl.pallas_call(functools.partial(forward_kernel, u), out_shape=(jax.Shape...]
    all_to_all x5 -> x0, local copies, waits for them, and re-layouts: 19.1 us -> none  [the longest x2 10.5 us: on_device(): lax.all_to_all(orbitals, 'orb', split_axis=2, concat_axis=0, tiled=True)]
    all_to_all x3 -> x0, starting transfers between devices: 13.7 us -> none  [the longest x1 5.33 us: on_device(): lax.all_to_all(orbitals, 'orb', split_axis=2, concat_axis=0, tiled=True)]
  transfers between devices with their start and end apart: 3 -> 19, of which waited for: 3 -> 6; matrix products, arithmetic and copies ran while one was open for 2% -> 9% of each run, Pallas kernels for 0% -> 4%
where the time goes in v1:
time: 116 us; the launch traced here: 115 us
  waiting for transfers between devices  37 us (32%)
  starting transfers between devices  30.8 us (27%)
  Pallas kernels  25.4 us (22%)
  other arithmetic  10.3 us (9%)
  local copies, waits for them, and re-layouts  7.55 us (7%)
  matrix products  1.99 us (2%)
  between operations  1.7 us (1%)
    ppermute x11, waiting for transfers between devices, swap(): return lax.ppermute(x, axes, moves)  29.5 us
    ppermute x8, starting transfers between devices, shift(): return lax.ppermute(x, axes, moves)  20.6 us
    ppermute x11, starting transfers between devices, swap(): return lax.ppermute(x, axes, moves)  10.3 us
    pallas_call x2, Pallas kernels, tile_device(): pl.pallas_call(functools.partial(forward_kernel, u), out_shape=(jax.Shape...  8.73 us
    pallas_call x2, Pallas kernels, tile_device(): pl.pallas_call(functools.partial(backward_kernel, u), out_shape=jax.Shape...  8.24 us
    ppermute x8, waiting for transfers between devices, shift(): return lax.ppermute(x, axes, moves)  7.46 us
    pallas_call x1, Pallas kernels, tile_device(): pl.pallas_call(rotate_kernel, out_shape=(part, part), in_specs=[VM] * 4,...  4.46 us
    pallas_call x1, Pallas kernels, tile_device(): pl.pallas_call(place_kernel, out_shape=jax.ShapeDtypeStruct(orbitals.shap...  4 us
  transfers between devices with their start and end apart: 19, of which 6 were waited for; matrix products, arithmetic and copies ran while one was open for 9% of the time, Pallas kernels for 4%

profile of v1, /device:TPU:0, one launch (start us, length us, event | category | flops | bytes accessed | tf_op | source)
XLA Modules:
  0.0 114.8 jit_solution(2671912730136323282)
XLA Ops:
  0.0 2.7 %slice_select_fusion = (f32[16,8,2048]{2,1,0:T(8,128)S(1)}, f32[16,8,2048]{2,1,0:T(8,128)}) fusion(f32[16,8,4096]{2,1,0:T(8,128)} %param.17, pred[]{:T(512)S(6)} %eq.87), kind=kLoop, calls=%fused_computation.4 | loop fusion | flops 524288 | bytes 4194305 | tf_op jit(solution)/shard_map/jit(_where)/select_n | solution.py:226
  2.7 0.5 collective-permute-start
  3.6 0.6 gather_fusion.1
  4.2 0.2 add_reduce_fusion.1
  4.9 0.3 fusion.8
  5.2 0.9 convolution_select_fusion.1.own
  6.1 0.9 convolution_select_fusion.sib
  6.9 1.0 copy-done.4
  7.9 4.5 %rotate.1 = (f32[16,8,2048]{2,1,0:T(8,128)}, f32[16,8,2048]{2,1,0:T(8,128)}) custom-call(f32[256,128]{1,0:T(8,128)} %convolution_select_fusion.1.own, f32[256,128]{1,0:T(8,128)} %convolution_select_fusion.sib, f32[16,8,2048]{2,1,0:T(8,128)} %get-tuple-element.25.mine, f32[16,8,2048]{2,1,0:T(8,128)} %copy-done.4), custom_call_target="tpu_custom_call" | custom-call | tf_op jit(solution)/shard_map/rotate/pallas_call | solution.py:253
  12.4 2.5 %collective-permute-start.1 = (f32[16,8,2048]{2,1,0:T(8,128)}, f32[16,8,2048]{2,1,0:T(8,128)S(1)}, u32[]{:S(2)}, u32[]{:S(2)}) collective-permute-start(f32[16,8,2048]{2,1,0:T(8,128)} %get-tuple-element.14), channel_id=1, source_target_pairs={{0,8},{1,9},{2,10},{3,11},{4,20},{5,21},{6,22},{7,23},{8,0},{9,1},... | collective-permute-start | bytes 3145736 | tf_op jit(solution)/shard_map/ppermute | solution.py:217
  14.8 13.0 %collective-permute-done.1 = f32[16,8,2048]{2,1,0:T(8,128)S(1)} collective-permute-done((f32[16,8,2048]{2,1,0:T(8,128)}, f32[16,8,2048]{2,1,0:T(8,128)S(1)}, u32[]{:S(2)}, u32[]{:S(2)}) %collective-permute-start.1) | collective-permute-done | bytes 1048608 | tf_op jit(solution)/shard_map/ppermute | solution.py:217
  27.8 1.3 %add.252 = f32[16,8,2048]{2,1,0:T(8,128)S(1)} add(f32[16,8,2048]{2,1,0:T(8,128)} %get-tuple-element.13, f32[16,8,2048]{2,1,0:T(8,128)S(1)} %collective-permute-done.1) | non-fusion elementwise | flops 262144 | bytes 3145728 | tf_op jit(solution)/shard_map/add | solution.py:256
  29.2 2.1 %collective-permute-start.2 = (f32[8,8,2048]{2,1,0:T(8,128)S(1)}, f32[8,8,2048]{2,1,0:T(8,128)S(1)}, u32[]{:S(2)}, u32[]{:S(2)}) collective-permute-start(f32[8,8,2048]{2,1,0:T(8,128)S(1)} %slice.48), channel_id=1, source_target_pairs={{0,16},{1,17},{2,18},{3,19},{4,12},{5,13},{6,14},{7,15},{8,24},{9,... | collective-permute-start | bytes 1572872 | tf_op jit(solution)/shard_map/ppermute | solution.py:217
  31.4 7.1 %collective-permute-done.2 = f32[8,8,2048]{2,1,0:T(8,128)S(1)} collective-permute-done((f32[8,8,2048]{2,1,0:T(8,128)S(1)}, f32[8,8,2048]{2,1,0:T(8,128)S(1)}, u32[]{:S(2)}, u32[]{:S(2)}) %collective-permute-start.2) | collective-permute-done | bytes 524320 | tf_op jit(solution)/shard_map/ppermute | solution.py:217
  38.7 0.6 pad_add_fusion.1.where
  39.7 1.5 %fusion.7 = (f32[512,128]{1,0:T(8,128)}, f32[512,128]{1,0:T(8,128)}, f32[512,128]{1,0:T(8,128)}, f32[512,128]{1,0:T(8,128)}, f32[512,128]{1,0:T(8,128)}, /*index=5*/f32[512,128]{1,0:T(8,128)}) fusion(f32[512]{0:T(512)S(1)} %mul.216, f32[64,128]{1,0:T(8,128)S(1)} %copy-done.16, f32[512]{0:T(512)S(1)} %mul.192, f32[64,128]{1,0:T(8,128)S(1)} %copy-done.17, ...), kind=kLoop, calls=%fused_computation.20 | loop fusion | flops 655360 | bytes 1646592 | tf_op jit(solution)/shard_map/mul | solution.py:270
  41.2 0.7 copy-done.2
  42.0 4.4 %forward_0.1 = (f32[512,256]{1,0:T(8,128)}, f32[64,256]{1,0:T(8,128)}, f32[64,256]{1,0:T(8,128)}) custom-call(s32[2]{0:T(128)} %pad_add_fusion.1.where, f32[8,8,2048]{2,1,0:T(8,128)} %copy-done.1, f32[6,8,2048]{2,1,0:T(8,128)} %copy-done.2, bf16[512,512]{1,0:T(8,128)(2,1)} %constant.126.clone.y_hi, bf16[512,512]{1,0:T(8,128)(2,1)} %constant.127.clone.y_lo, ...), custom_call_target="tpu_custom_call" | custom-call | tf_op jit(solution)/shard_map/forward_0/pallas_call | solution.py:288
  46.3 1.4 %collective-permute-start.6 = (f32[64,256]{1,0:T(8,128)}, f32[64,256]{1,0:T(8,128)S(1)}, u32[]{:S(2)}, u32[]{:S(2)}) collective-permute-start(f32[64,256]{1,0:T(8,128)} %get-tuple-element.17), channel_id=1, source_target_pairs={{1,0},{2,1},{3,2},{5,4},{6,5},{7,6},{9,8},{10,9},{11,10},{13,12},{... | collective-permute-start | bytes 196616 | tf_op jit(solution)/shard_map/ppermute | solution.py:222
  47.8 4.4 %forward_1.1 = (f32[512,256]{1,0:T(8,128)}, f32[64,256]{1,0:T(8,128)}, f32[64,256]{1,0:T(8,128)}) custom-call(s32[2]{0:T(128)} %pad_add_fusion.1.where, f32[8,8,2048]{2,1,0:T(8,128)} %copy-done.1, f32[6,8,2048]{2,1,0:T(8,128)} %copy-done.2, bf16[512,512]{1,0:T(8,128)(2,1)} %constant.126.clone.y_hi, bf16[512,512]{1,0:T(8,128)(2,1)} %constant.127.clone.y_lo, ...), custom_call_target="tpu_custom_call" | custom-call | tf_op jit(solution)/shard_map/forward_1/pallas_call | solution.py:288
  52.1 4.6 %collective-permute-start.8 = (f32[64,256]{1,0:T(8,128)}, f32[64,256]{1,0:T(8,128)S(1)}, u32[]{:S(2)}, u32[]{:S(2)}) collective-permute-start(f32[64,256]{1,0:T(8,128)} %get-tuple-element.19), channel_id=1, source_target_pairs={{0,1},{1,2},{2,3},{4,5},{5,6},{6,7},{8,9},{9,10},{10,11},{12,13},{... | collective-permute-start | bytes 196616 | tf_op jit(solution)/shard_map/ppermute | solution.py:222
  56.8 3.9 %collective-permute-start.4 = (f32[64,256]{1,0:T(8,128)S(1)}, f32[64,256]{1,0:T(8,128)S(1)}, u32[]{:S(2)}, u32[]{:S(2)}) collective-permute-start(f32[64,256]{1,0:T(8,128)S(1)} %copy-done.14), channel_id=1, source_target_pairs={{0,1},{1,2},{2,3},{4,5},{5,6},{6,7},{8,9},{9,10},{10,11},{12,13},{... | collective-permute-start | bytes 196616 | tf_op jit(solution)/shard_map/ppermute | solution.py:222
  60.7 1.3 %collective-permute-start.10 = (f32[64,256]{1,0:T(8,128)}, f32[64,256]{1,0:T(8,128)S(1)}, u32[]{:S(2)}, u32[]{:S(2)}) collective-permute-start(f32[64,256]{1,0:T(8,128)} %get-tuple-element.20), channel_id=1, source_target_pairs={{1,0},{2,1},{3,2},{5,4},{6,5},{7,6},{9,8},{10,9},{11,10},{13,12},{... | collective-permute-start | bytes 196616 | tf_op jit(solution)/shard_map/ppermute | solution.py:222
  62.0 0.6 fusion.15
  63.9 3.1 %collective-permute-done.10 = f32[64,256]{1,0:T(8,128)S(1)} collective-permute-done((f32[64,256]{1,0:T(8,128)}, f32[64,256]{1,0:T(8,128)S(1)}, u32[]{:S(2)}, u32[]{:S(2)}) %collective-permute-start.10) | collective-permute-done | bytes 65568 | tf_op jit(solution)/shard_map/ppermute | solution.py:222
  67.1 0.9 multiply_add_fusion.5
  68.0 1.3 %collective-permute-start.7 = (f32[64,256]{1,0:T(8,128)S(1)}, f32[64,256]{1,0:T(8,128)S(1)}, u32[]{:S(2)}, u32[]{:S(2)}) collective-permute-start(f32[64,256]{1,0:T(8,128)S(1)} %get-tuple-element.34), channel_id=1, source_target_pairs={{2,0},{3,1},{6,4},{7,5},{10,8},{11,9},{14,12},{15,13},{18,16},{19,... | collective-permute-start | bytes 196616 | tf_op jit(solution)/shard_map/ppermute | solution.py:222
  69.3 5.4 %collective-permute-start.9 = (f32[64,256]{1,0:T(8,128)S(1)}, f32[64,256]{1,0:T(8,128)S(1)}, u32[]{:S(2)}, u32[]{:S(2)}) collective-permute-start(f32[64,256]{1,0:T(8,128)S(1)} %get-tuple-element.35), channel_id=1, source_target_pairs={{0,2},{1,3},{4,6},{5,7},{8,10},{9,11},{12,14},{13,15},{16,18},{17,... | collective-permute-start | bytes 196616 | tf_op jit(solution)/shard_map/ppermute | solution.py:222
  74.7 1.3 %collective-permute-start.5 = (f32[64,256]{1,0:T(8,128)S(1)}, f32[64,256]{1,0:T(8,128)S(1)}, u32[]{:S(2)}, u32[]{:S(2)}) collective-permute-start(f32[64,256]{1,0:T(8,128)S(1)} %get-tuple-element.36), channel_id=1, source_target_pairs={{0,2},{1,3},{4,6},{5,7},{8,10},{9,11},{12,14},{13,15},{16,18},{17,... | collective-permute-start | bytes 196616 | tf_op jit(solution)/shard_map/ppermute | solution.py:222
  76.0 1.3 %collective-permute-start.11 = (f32[64,256]{1,0:T(8,128)S(1)}, f32[64,256]{1,0:T(8,128)S(1)}, u32[]{:S(2)}, u32[]{:S(2)}) collective-permute-start(f32[64,256]{1,0:T(8,128)S(1)} %get-tuple-element.37), channel_id=1, source_target_pairs={{2,0},{3,1},{6,4},{7,5},{10,8},{11,9},{14,12},{15,13},{18,16},{19,... | collective-permute-start | bytes 196616 | tf_op jit(solution)/shard_map/ppermute | solution.py:222
  77.3 0.8 dynamic-slice_convert_fusion
  78.1 0.7 reshape.371.flags
  78.8 4.3 %collective-permute-done.11 = f32[64,256]{1,0:T(8,128)S(1)} collective-permute-done((f32[64,256]{1,0:T(8,128)S(1)}, f32[64,256]{1,0:T(8,128)S(1)}, u32[]{:S(2)}, u32[]{:S(2)}) %collective-permute-start.11) | collective-permute-done | bytes 65568 | tf_op jit(solution)/shard_map/ppermute | solution.py:222
  83.1 0.7 multiply_add_fusion.4
  83.8 4.1 %backward_1.1 = f32[8,4096]{1,0:T(8,128)} custom-call(s32[2]{0:T(128)} %pad_add_fusion.1.where, f32[8]{0:T(128)} %reshape.371.flags, f32[8,8,2048]{2,1,0:T(8,128)} %copy-done.1, f32[6,8,2048]{2,1,0:T(8,128)} %copy-done.2, bf16[512,512]{1,0:T(8,128)(2,1)} %constant.126.clone.y_hi, bf16[512,512]{1,0:T(8,128)(2,1)} %constant.127.clone.y_lo, ...), custom_call_target="tpu_custom_call" | custom-call | tf_op jit(solution)/shard_map/backward_1/pallas_call | solution.py:313
  87.9 4.1 %backward_0.1 = f32[8,4096]{1,0:T(8,128)} custom-call(s32[2]{0:T(128)} %pad_add_fusion.1.where, f32[8]{0:T(128)} %reshape.371.flags, f32[8,8,2048]{2,1,0:T(8,128)} %copy-done.1, f32[6,8,2048]{2,1,0:T(8,128)} %copy-done.2, bf16[512,512]{1,0:T(8,128)(2,1)} %constant.126.clone.y_hi, bf16[512,512]{1,0:T(8,128)(2,1)} %constant.127.clone.y_lo, ...), custom_call_target="tpu_custom_call" | custom-call | tf_op jit(solution)/shard_map/backward_0/pallas_call | solution.py:313
  92.1 0.9 pad_maximum_fusion.refs_0_
  93.0 1.6 %collective-permute-start.12 = (f32[2,8,4096]{2,1,0:T(8,128)S(1)}, f32[2,8,4096]{2,1,0:T(8,128)S(1)}, u32[]{:S(2)}, u32[]{:S(2)}) collective-permute-start(f32[2,8,4096]{2,1,0:T(8,128)S(1)} %pad_maximum_fusion.refs_0_), channel_id=1, source_target_pairs={{0,8},{1,9},{2,10},{3,11},{4,20},{5,21},{6,22},{7,23},{8,0},{9,1},... | collective-permute-start | bytes 786440 | tf_op jit(solution)/shard_map/ppermute | solution.py:217
  94.8 1.5 %collective-permute-start.13 = (f32[2,8,4096]{2,1,0:T(8,128)S(1)}, f32[2,8,4096]{2,1,0:T(8,128)S(1)}, u32[]{:S(2)}, u32[]{:S(2)}) collective-permute-start(f32[2,8,4096]{2,1,0:T(8,128)S(1)} %pad_maximum_fusion.refs_0_), channel_id=1, source_target_pairs={{0,16},{1,17},{2,18},{3,19},{4,12},{5,13},{6,14},{7,15},{8,24},{9,... | collective-permute-start | bytes 786440 | tf_op jit(solution)/shard_map/ppermute | solution.py:217
  96.3 5.0 %collective-permute-done.12.refs_1_ = f32[2,8,4096]{2,1,0:T(8,128)S(1)} collective-permute-done((f32[2,8,4096]{2,1,0:T(8,128)S(1)}, f32[2,8,4096]{2,1,0:T(8,128)S(1)}, u32[]{:S(2)}, u32[]{:S(2)}) %collective-permute-start.12) | collective-permute-done | bytes 262176 | tf_op jit(solution)/shard_map/ppermute | solution.py:217
  101.3 1.4 %collective-permute-start.14 = (f32[2,8,4096]{2,1,0:T(8,128)S(1)}, f32[2,8,4096]{2,1,0:T(8,128)S(1)}, u32[]{:S(2)}, u32[]{:S(2)}) collective-permute-start(f32[2,8,4096]{2,1,0:T(8,128)S(1)} %collective-permute-done.12.refs_1_), channel_id=1, source_target_pairs={{0,16},{1,17},{2,18},{3,19},{4,12},{5,13},{6,14},{7,15},{8,24},{9,... | collective-permute-start | bytes 786440 | tf_op jit(solution)/shard_map/ppermute | solution.py:217
  102.8 0.5 collective-permute-start.16
  103.4 4.3 %collective-permute-done.14.refs_3_ = f32[2,8,4096]{2,1,0:T(8,128)S(1)} collective-permute-done((f32[2,8,4096]{2,1,0:T(8,128)S(1)}, f32[2,8,4096]{2,1,0:T(8,128)S(1)}, u32[]{:S(2)}, u32[]{:S(2)}) %collective-permute-start.14) | collective-permute-done | bytes 262176 | tf_op jit(solution)/shard_map/ppermute | solution.py:217
  107.7 0.6 gather_fusion
  108.5 0.7 reshape.373.match
  109.3 0.6 copy-done.9
  110.1 0.7 copy-done.12
  110.8 4.0 %place.1 = f32[16,8,4096]{2,1,0:T(8,128)} custom-call(f32[32]{0:T(128)} %reshape.373.match, f32[2,8,4096]{2,1,0:T(8,128)} %copy-done.3, f32[2,8,4096]{2,1,0:T(8,128)} %copy-done.6, f32[2,8,4096]{2,1,0:T(8,128)} %copy-done.7, f32[2,8,4096]{2,1,0:T(8,128)} %copy-done.8, f32[2,8,4096]{2,1,0:T(8,128)} %copy-done.9, f32[2,8,4096]{2,1,0:T(8,128)} %copy-done.10, ...), custom_call_target="tpu_custom_call" | custom-call | tf_op jit(solution)/shard_map/place/pallas_call | solution.py:335
  (88 shorter events, 2.4 us)
Async XLA Ops:
  0.0 4.9 %copy-start = (f32[128,128]{1,0:T(8,128)S(1)}, f32[128,128]{1,0:T(8,128)}, u32[]{:S(2)}) copy-start(f32[128,128]{1,0:T(8,128)} %param.18) | copy-start | bytes 196612
  0.0 3.2 %copy-start.18 = (s32[4,2]{0,1:T(2,128)S(1)}, s32[4,2]{0,1:T(2,128)}, u32[]{:S(2)}) copy-start(s32[4,2]{0,1:T(2,128)} %param.19) | copy-start | bytes 100
  2.7 4.2 %collective-permute-start = (f32[16,8,2048]{2,1,0:T(8,128)S(1)}, f32[16,8,2048]{2,1,0:T(8,128)S(1)}, u32[]{:S(2)}, u32[]{:S(2)}) collective-permute-start(f32[16,8,2048]{2,1,0:T(8,128)S(1)} %get-tuple-element.24), channel_id=1, source_target_pairs={{0,4},{1,5},{2,6},{3,7},{4,0},{5,1},{6,2},{7,3},{8,12},{9,13},{10,... | collective-permute-start | bytes 3145736 | tf_op jit(solution)/shard_map/ppermute | solution.py:217
  6.9 1.0 copy-start.4
  12.4 15.5 %collective-permute-start.1 = (f32[16,8,2048]{2,1,0:T(8,128)}, f32[16,8,2048]{2,1,0:T(8,128)S(1)}, u32[]{:S(2)}, u32[]{:S(2)}) collective-permute-start(f32[16,8,2048]{2,1,0:T(8,128)} %get-tuple-element.14), channel_id=1, source_target_pairs={{0,8},{1,9},{2,10},{3,11},{4,20},{5,21},{6,22},{7,23},{8,0},{9,1},... | collective-permute-start | bytes 3145736 | tf_op jit(solution)/shard_map/ppermute | solution.py:217
  29.2 10.6 %copy-start.16 = (f32[64,128]{1,0:T(8,128)S(1)}, f32[64,128]{1,0:T(8,128)}, u32[]{:S(2)}) copy-start(f32[64,128]{1,0:T(8,128)} %constant.123.clone) | copy-start | bytes 98308
  29.2 10.6 %copy-start.17 = (f32[64,128]{1,0:T(8,128)S(1)}, f32[64,128]{1,0:T(8,128)}, u32[]{:S(2)}) copy-start(f32[64,128]{1,0:T(8,128)} %constant.124.clone) | copy-start | bytes 98308
  29.2 9.3 %collective-permute-start.2 = (f32[8,8,2048]{2,1,0:T(8,128)S(1)}, f32[8,8,2048]{2,1,0:T(8,128)S(1)}, u32[]{:S(2)}, u32[]{:S(2)}) collective-permute-start(f32[8,8,2048]{2,1,0:T(8,128)S(1)} %slice.48), channel_id=1, source_target_pairs={{0,16},{1,17},{2,18},{3,19},{4,12},{5,13},{6,14},{7,15},{8,24},{9,... | collective-permute-start | bytes 1572872 | tf_op jit(solution)/shard_map/ppermute | solution.py:217
  38.6 2.6 %copy-start.1 = (f32[8,8,2048]{2,1,0:T(8,128)}, f32[8,8,2048]{2,1,0:T(8,128)S(1)}, u32[]{:S(2)}) copy-start(f32[8,8,2048]{2,1,0:T(8,128)S(1)} %slice_add_fusion.own) | copy-start | bytes 1572868
  38.6 2.6 %collective-permute-start.3 = (f32[6,8,2048]{2,1,0:T(8,128)S(1)}, f32[6,8,2048]{2,1,0:T(8,128)S(1)}, u32[]{:S(2)}, u32[]{:S(2)}) collective-permute-start(f32[6,8,2048]{2,1,0:T(8,128)S(1)} %slice.49), channel_id=1, source_target_pairs={{0,4},{1,5},{2,6},{3,7},{4,0},{5,1},{6,2},{7,3},{8,12},{9,13},{10,... | collective-permute-start | bytes 1179656 | tf_op jit(solution)/shard_map/ppermute | solution.py:217
  41.2 0.7 copy-start.2
  46.3 10.4 %copy-start.14 = (f32[64,256]{1,0:T(8,128)S(1)}, f32[64,256]{1,0:T(8,128)}, u32[]{:S(2)}) copy-start(f32[64,256]{1,0:T(8,128)} %get-tuple-element.16) | copy-start | bytes 196612
  46.3 20.7 %copy-start.13 = (f32[64,256]{1,0:T(8,128)S(1)}, f32[64,256]{1,0:T(8,128)}, u32[]{:S(2)}) copy-start(f32[64,256]{1,0:T(8,128)} %constant.132.clone) | copy-start | bytes 196612
  46.3 20.7 %copy-start.15 = (f32[64,256]{1,0:T(8,128)S(1)}, f32[64,256]{1,0:T(8,128)}, u32[]{:S(2)}) copy-start(f32[64,256]{1,0:T(8,128)} %get-tuple-element.17) | copy-start | bytes 196612
  46.3 17.6 %collective-permute-start.6 = (f32[64,256]{1,0:T(8,128)}, f32[64,256]{1,0:T(8,128)S(1)}, u32[]{:S(2)}, u32[]{:S(2)}) collective-permute-start(f32[64,256]{1,0:T(8,128)} %get-tuple-element.17), channel_id=1, source_target_pairs={{1,0},{2,1},{3,2},{5,4},{6,5},{7,6},{9,8},{10,9},{11,10},{13,12},{... | collective-permute-start | bytes 196616 | tf_op jit(solution)/shard_map/ppermute | solution.py:222
  52.1 11.8 %collective-permute-start.8 = (f32[64,256]{1,0:T(8,128)}, f32[64,256]{1,0:T(8,128)S(1)}, u32[]{:S(2)}, u32[]{:S(2)}) collective-permute-start(f32[64,256]{1,0:T(8,128)} %get-tuple-element.19), channel_id=1, source_target_pairs={{0,1},{1,2},{2,3},{4,5},{5,6},{6,7},{8,9},{9,10},{10,11},{12,13},{... | collective-permute-start | bytes 196616 | tf_op jit(solution)/shard_map/ppermute | solution.py:222
  56.8 7.2 %collective-permute-start.4 = (f32[64,256]{1,0:T(8,128)S(1)}, f32[64,256]{1,0:T(8,128)S(1)}, u32[]{:S(2)}, u32[]{:S(2)}) collective-permute-start(f32[64,256]{1,0:T(8,128)S(1)} %copy-done.14), channel_id=1, source_target_pairs={{0,1},{1,2},{2,3},{4,5},{5,6},{6,7},{8,9},{9,10},{10,11},{12,13},{... | collective-permute-start | bytes 196616 | tf_op jit(solution)/shard_map/ppermute | solution.py:222
  60.7 6.4 %collective-permute-start.10 = (f32[64,256]{1,0:T(8,128)}, f32[64,256]{1,0:T(8,128)S(1)}, u32[]{:S(2)}, u32[]{:S(2)}) collective-permute-start(f32[64,256]{1,0:T(8,128)} %get-tuple-element.20), channel_id=1, source_target_pairs={{1,0},{2,1},{3,2},{5,4},{6,5},{7,6},{9,8},{10,9},{11,10},{13,12},{... | collective-permute-start | bytes 196616 | tf_op jit(solution)/shard_map/ppermute | solution.py:222
  68.0 10.8 %collective-permute-start.7 = (f32[64,256]{1,0:T(8,128)S(1)}, f32[64,256]{1,0:T(8,128)S(1)}, u32[]{:S(2)}, u32[]{:S(2)}) collective-permute-start(f32[64,256]{1,0:T(8,128)S(1)} %get-tuple-element.34), channel_id=1, source_target_pairs={{2,0},{3,1},{6,4},{7,5},{10,8},{11,9},{14,12},{15,13},{18,16},{19,... | collective-permute-start | bytes 196616 | tf_op jit(solution)/shard_map/ppermute | solution.py:222
  69.3 9.5 %collective-permute-start.9 = (f32[64,256]{1,0:T(8,128)S(1)}, f32[64,256]{1,0:T(8,128)S(1)}, u32[]{:S(2)}, u32[]{:S(2)}) collective-permute-start(f32[64,256]{1,0:T(8,128)S(1)} %get-tuple-element.35), channel_id=1, source_target_pairs={{0,2},{1,3},{4,6},{5,7},{8,10},{9,11},{12,14},{13,15},{16,18},{17,... | collective-permute-start | bytes 196616 | tf_op jit(solution)/shard_map/ppermute | solution.py:222
  74.7 4.0 %collective-permute-start.5 = (f32[64,256]{1,0:T(8,128)S(1)}, f32[64,256]{1,0:T(8,128)S(1)}, u32[]{:S(2)}, u32[]{:S(2)}) collective-permute-start(f32[64,256]{1,0:T(8,128)S(1)} %get-tuple-element.36), channel_id=1, source_target_pairs={{0,2},{1,3},{4,6},{5,7},{8,10},{9,11},{12,14},{13,15},{16,18},{17,... | collective-permute-start | bytes 196616 | tf_op jit(solution)/shard_map/ppermute | solution.py:222
  76.0 7.1 %collective-permute-start.11 = (f32[64,256]{1,0:T(8,128)S(1)}, f32[64,256]{1,0:T(8,128)S(1)}, u32[]{:S(2)}, u32[]{:S(2)}) collective-permute-start(f32[64,256]{1,0:T(8,128)S(1)} %get-tuple-element.37), channel_id=1, source_target_pairs={{2,0},{3,1},{6,4},{7,5},{10,8},{11,9},{14,12},{15,13},{18,16},{19,... | collective-permute-start | bytes 196616 | tf_op jit(solution)/shard_map/ppermute | solution.py:222
  87.9 4.1 %copy-start.5 = (f32[8,4096]{1,0:T(8,128)S(1)}, f32[8,4096]{1,0:T(8,128)}, u32[]{:S(2)}) copy-start(f32[8,4096]{1,0:T(8,128)} %backward_1.1) | copy-start | bytes 393220
  93.0 16.3 %copy-start.3 = (f32[2,8,4096]{2,1,0:T(8,128)}, f32[2,8,4096]{2,1,0:T(8,128)S(1)}, u32[]{:S(2)}) copy-start(f32[2,8,4096]{2,1,0:T(8,128)S(1)} %pad_maximum_fusion.refs_0_) | copy-start | bytes 786436
  93.0 8.3 %collective-permute-start.12 = (f32[2,8,4096]{2,1,0:T(8,128)S(1)}, f32[2,8,4096]{2,1,0:T(8,128)S(1)}, u32[]{:S(2)}, u32[]{:S(2)}) collective-permute-start(f32[2,8,4096]{2,1,0:T(8,128)S(1)} %pad_maximum_fusion.refs_0_), channel_id=1, source_target_pairs={{0,8},{1,9},{2,10},{3,11},{4,20},{5,21},{6,22},{7,23},{8,0},{9,1},... | collective-permute-start | bytes 786440 | tf_op jit(solution)/shard_map/ppermute | solution.py:217
  94.8 8.5 %collective-permute-start.13 = (f32[2,8,4096]{2,1,0:T(8,128)S(1)}, f32[2,8,4096]{2,1,0:T(8,128)S(1)}, u32[]{:S(2)}, u32[]{:S(2)}) collective-permute-start(f32[2,8,4096]{2,1,0:T(8,128)S(1)} %pad_maximum_fusion.refs_0_), channel_id=1, source_target_pairs={{0,16},{1,17},{2,18},{3,19},{4,12},{5,13},{6,14},{7,15},{8,24},{9,... | collective-permute-start | bytes 786440 | tf_op jit(solution)/shard_map/ppermute | solution.py:217
  101.3 7.9 %copy-start.6 = (f32[2,8,4096]{2,1,0:T(8,128)}, f32[2,8,4096]{2,1,0:T(8,128)S(1)}, u32[]{:S(2)}) copy-start(f32[2,8,4096]{2,1,0:T(8,128)S(1)} %collective-permute-done.12.refs_1_) | copy-start | bytes 786436
  101.3 6.4 %collective-permute-start.14 = (f32[2,8,4096]{2,1,0:T(8,128)S(1)}, f32[2,8,4096]{2,1,0:T(8,128)S(1)}, u32[]{:S(2)}, u32[]{:S(2)}) collective-permute-start(f32[2,8,4096]{2,1,0:T(8,128)S(1)} %collective-permute-done.12.refs_1_), channel_id=1, source_target_pairs={{0,16},{1,17},{2,18},{3,19},{4,12},{5,13},{6,14},{7,15},{8,24},{9,... | collective-permute-start | bytes 786440 | tf_op jit(solution)/shard_map/ppermute | solution.py:217
  102.7 6.5 %collective-permute-start.15 = (f32[2,8,4096]{2,1,0:T(8,128)S(1)}, f32[2,8,4096]{2,1,0:T(8,128)S(1)}, u32[]{:S(2)}, u32[]{:S(2)}) collective-permute-start(f32[2,8,4096]{2,1,0:T(8,128)S(1)} %pad_maximum_fusion.refs_0_), channel_id=1, source_target_pairs={{0,4},{1,5},{2,6},{3,7},{4,0},{5,1},{6,2},{7,3},{8,12},{9,13},{10,... | collective-permute-start | bytes 786440 | tf_op jit(solution)/shard_map/ppermute | solution.py:217
  102.8 6.4 %collective-permute-start.16 = (f32[2,8,4096]{2,1,0:T(8,128)S(1)}, f32[2,8,4096]{2,1,0:T(8,128)S(1)}, u32[]{:S(2)}, u32[]{:S(2)}) collective-permute-start(f32[2,8,4096]{2,1,0:T(8,128)S(1)} %collective-permute-done.12.refs_1_), channel_id=1, source_target_pairs={{0,4},{1,5},{2,6},{3,7},{4,0},{5,1},{6,2},{7,3},{8,12},{9,13},{10,... | collective-permute-start | bytes 786440 | tf_op jit(solution)/shard_map/ppermute | solution.py:217
  103.3 6.0 %copy-start.7 = (f32[2,8,4096]{2,1,0:T(8,128)}, f32[2,8,4096]{2,1,0:T(8,128)S(1)}, u32[]{:S(2)}) copy-start(f32[2,8,4096]{2,1,0:T(8,128)S(1)} %collective-permute-done.13.refs_2_) | copy-start | bytes 786436
  103.3 5.9 %collective-permute-start.17 = (f32[2,8,4096]{2,1,0:T(8,128)S(1)}, f32[2,8,4096]{2,1,0:T(8,128)S(1)}, u32[]{:S(2)}, u32[]{:S(2)}) collective-permute-start(f32[2,8,4096]{2,1,0:T(8,128)S(1)} %collective-permute-done.13.refs_2_), channel_id=1, source_target_pairs={{0,4},{1,5},{2,6},{3,7},{4,0},{5,1},{6,2},{7,3},{8,12},{9,13},{10,... | collective-permute-start | bytes 786440 | tf_op jit(solution)/shard_map/ppermute | solution.py:217
  107.7 1.6 %copy-start.8 = (f32[2,8,4096]{2,1,0:T(8,128)}, f32[2,8,4096]{2,1,0:T(8,128)S(1)}, u32[]{:S(2)}) copy-start(f32[2,8,4096]{2,1,0:T(8,128)S(1)} %collective-permute-done.14.refs_3_) | copy-start | bytes 786436
  107.7 1.5 %collective-permute-start.18 = (f32[2,8,4096]{2,1,0:T(8,128)S(1)}, f32[2,8,4096]{2,1,0:T(8,128)S(1)}, u32[]{:S(2)}, u32[]{:S(2)}) collective-permute-start(f32[2,8,4096]{2,1,0:T(8,128)S(1)} %collective-permute-done.14.refs_3_), channel_id=1, source_target_pairs={{0,4},{1,5},{2,6},{3,7},{4,0},{5,1},{6,2},{7,3},{8,12},{9,13},{10,... | collective-permute-start | bytes 786440 | tf_op jit(solution)/shard_map/ppermute | solution.py:217
  109.2 0.7 copy-start.9
  109.2 0.8 copy-start.10
  109.2 0.9 copy-start.11
  110.1 0.7 copy-start.12

commit v2 on v1

--- a/solution.py
+++ b/solution.py
@@ -88,7 +88,8 @@
 
 
 def forward_kernel(u, where, own, other, y_hi, y_lo, z_hi, z_lo, decay, left, right, k_left, k_right,
-                   local, a_out, b_out, dens, work, fwd, bwd):
+                   local, *rest):
+    messages, (dens, work, fwd, bwd) = rest[:-4], rest[-4:]
     tiles = own.shape[2] // LANES
     core = where[0]
     for side, ref, source, target in ((0, own, BLK // 2, BLK // 2 + BLK + u), (1, other, 2, u)):
@@ -132,14 +133,18 @@
         return carry
 
     lax.fori_loop(0, NY, solve, 0, unroll=4)
+    g = where[1]
     for q in range(BLK // 2):
         lanes = slice(q * LANES, (q + 1) * LANES)
-        a_out[:, lanes] = fwd[q, pl.ds(SUB - 1, NY, stride=SUB), :]
-        b_out[:, lanes] = bwd[q, pl.ds(0, NY, stride=SUB), :]
-
-
-def backward_kernel(u, where, flags, own, other, y_hi, y_lo, z_hi, z_lo, local, from_left, from_right,
-                    in_left, in_right, out, work, pot):
+        rightward = fwd[q, pl.ds(SUB - 1, NY, stride=SUB), :]
+        leftward = bwd[q, pl.ds(0, NY, stride=SUB), :]
+        for k, out in enumerate(messages, 1):
+            out[:, lanes] = jnp.where((g ^ k) > g, rightward, leftward)
+
+
+def backward_kernel(u, where, flags, own, other, y_hi, y_lo, z_hi, z_lo, local, in_left, in_right, slab, *rest):
+    received, (out, work, pot) = rest[:-3], rest[-3:]
+    g = where[1]
     tiles = own.shape[2] // LANES
     core = where[0]
 
@@ -147,7 +152,20 @@
         lines = pl.ds(pl.multiple_of(group * SUB, SUB), SUB)
         for q in range(BLK // 2):
             lanes = slice(q * LANES, (q + 1) * LANES)
-            lp, rp = from_left[lines, lanes], from_right[lines, lanes]
+            lp = rp = jnp.zeros((SUB, LANES), f32)
+            powers = [jnp.ones((SUB, LANES), f32), slab[lines, :]]
+            while len(powers) < len(received):
+                powers.append(powers[-1] * powers[1])
+            for n, ref in enumerate(received, 1):
+                peer = g ^ n
+                distance = jnp.abs(peer - g)
+                value = ref[lines, lanes]
+                factor = powers[n - 1]
+                for d in range(1, n):
+                    factor = jnp.where(distance == d, powers[d - 1], factor)
+                value = factor * value
+                lp = lp + jnp.where(peer < g, value, 0.0)
+                rp = rp + jnp.where(peer < g, 0.0, value)
             for k in range(SUB):
                 rows = pl.ds(pl.multiple_of((group * SUB + k) * SUB, SUB), SUB)
                 here = in_left[rows, :] * lp[k:k + 1] + in_right[rows, :] * rp[k:k + 1]
@@ -216,9 +234,8 @@
             moves += [(a * n_grid + b, (a ^ flip) * n_grid + b) for b in range(n_grid)]
         return lax.ppermute(x, axes, moves)
 
-    def shift(x, step):
-        moves = [(a * n_grid + b, a * n_grid + b + step) for a in range(n_orb)
-                 for b in range(n_grid) if 0 <= b + step < n_grid]
+    def cross(x, k):
+        moves = [(a * n_grid + b, a * n_grid + (b ^ k)) for a in range(n_orb) for b in range(n_grid)]
         return lax.ppermute(x, axes, moves)
 
     low, high = orbitals[:, :, :half], orbitals[:, :, half:]
@@ -270,7 +287,7 @@
     in_right = (k_right * jnp.exp((planes - p) * log_r)).reshape(-1, LANES)
     left, right, k_left, k_right = (v.reshape(-1, LANES) for v in (left, right, k_left, k_right))
     spread_decay = jnp.asarray(np.repeat(decay, SUB, axis=0), f32)
-    slab = np.concatenate([decay, decay], axis=1) ** planes
+    slab = jnp.asarray(decay**planes, f32)
 
     y_hi, y_lo = halves_np(y_table())
     z_hi, z_lo = halves_np(z_table())
@@ -285,39 +302,27 @@
     for u in range(BLK // 2):
         lines = jax.ShapeDtypeStruct((NY, 2 * LANES), f32)
         cube = (NY * SUB, 2 * LANES)
-        local, a, b = pl.pallas_call(
+        local, *messages = pl.pallas_call(
             functools.partial(forward_kernel, u),
-            out_shape=(jax.ShapeDtypeStruct(cube, f32), lines, lines),
+            out_shape=[jax.ShapeDtypeStruct(cube, f32)] + [lines] * (n_grid - 1),
             in_specs=[SM] + [VM] * 11,
-            out_specs=(VM, VM, VM),
+            out_specs=[VM] * n_grid,
             scratch_shapes=[pltpu.VMEM((width // LANES * SUB, BLK * LANES), f32), pltpu.VMEM(cube, f32)]
             + [pltpu.VMEM((BLK // 2, NY * SUB, LANES), f32)] * 2,
             name=f"forward_{u}",
         )(where, own, other, y_hi, y_lo, z_hi, z_lo, spread_decay, left, right, k_left, k_right)
-        from_left = from_right = None
-        step = 1
-        while step < n_grid:
-            got_a, got_b = shift(a, step), shift(b, -step)
-            if from_left is None:
-                from_left, from_right = got_a, got_b
-            else:
-                factor = jnp.asarray(slab ** (step - 1), f32)
-                from_left, from_right = from_left + factor * got_a, from_right + factor * got_b
-            factor = jnp.asarray(slab**step, f32)
-            a, b = a + factor * got_a, b + factor * got_b
-            step *= 2
-        solved.append((local, from_left, from_right))
+        solved.append((local, [cross(m, k) for k, m in enumerate(messages, 1)]))
 
     terms = []
-    for u, (local, from_left, from_right) in enumerate(solved):
+    for u, (local, received) in enumerate(solved):
         terms.append(pl.pallas_call(
             functools.partial(backward_kernel, u),
             out_shape=jax.ShapeDtypeStruct((planes, width), f32),
-            in_specs=[SM, SM] + [VM] * 11,
+            in_specs=[SM, SM] + [VM] * (9 + n_grid),
             out_specs=VM,
             scratch_shapes=[pltpu.VMEM(cube, f32), pltpu.VMEM((width // LANES * SUB, BLK * LANES), f32)],
             name=f"backward_{u}",
-        )(where, flags, own, other, y_hi, y_lo, zt_hi, zt_lo, local, from_left, from_right, in_left, in_right))
+        )(where, flags, own, other, y_hi, y_lo, zt_hi, zt_lo, local, in_left, in_right, slab, *received))
 
     term = jnp.stack(terms)
     near_1 = swap(term, 2, 4)
@@ -438,7 +443,7 @@
     def on_device(orbitals, rotation, tile_list, pair_mask):
         per_device, planes, width = orbitals.shape
         fits = n_orb == 8 and 2 * tile_list.shape[0] == n_orb and planes == SUB and per_device % BLK == 0
-        fits = fits and width == NY * NZ and 2 * NZ == LANES
+        fits = fits and width == NY * NZ and 2 * NZ == LANES and n_grid in (2, 4, 8)
         body = tile_device if fits else any_device
         return body(orbitals, rotation, tile_list, pair_mask)
 

time: 116 us -> 97.3 us (0.84)
  starting transfers between devices: 30.8 us -> 18.8 us
  waiting for transfers between devices: 37 us -> 31.1 us
  other arithmetic: 10.3 us -> 8.83 us
  local copies, waits for them, and re-layouts: 7.55 us -> 8.76 us
    ppermute x8 -> x6, starting transfers between devices: 20.6 us -> 9.12 us  [cross(): return lax.ppermute(x, axes, moves)]
    ppermute x8 -> x6, waiting for transfers between devices: 7.46 us -> 0.02 us  [cross(): return lax.ppermute(x, axes, moves)]
    add x2 -> x0, other arithmetic: 1.64 us -> none  [the longest x1 0.91 us: tile_device(): a, b = (a + factor * got_a, b + factor * got_b)]
    ppermute x11, waiting for transfers between devices: 29.5 us -> 31.1 us  [swap(): return lax.ppermute(x, axes, moves)]
    unnamed x39 -> x45, local copies, waits for them, and re-layouts: 3.37 us -> 4.63 us
  transfers between devices with their start and end apart: 19 -> 17, of which waited for: 6 -> 4; matrix products, arithmetic and copies ran while one was open for 9% -> 10% of each run, Pallas kernels for 4% -> 9%
where the time goes in v2:
time: 97.3 us; the launch traced here: 96.7 us
  waiting for transfers between devices  31.1 us (32%)
  Pallas kernels  25.7 us (26%)
  starting transfers between devices  18.8 us (19%)
  other arithmetic  8.83 us (9%)
  local copies, waits for them, and re-layouts  8.76 us (9%)
  matrix products  2 us (2%)
  between operations  1.6 us (2%)
    ppermute x11, waiting for transfers between devices, swap(): return lax.ppermute(x, axes, moves)  31.1 us
    ppermute x11, starting transfers between devices, swap(): return lax.ppermute(x, axes, moves)  9.63 us
    ppermute x6, starting transfers between devices, cross(): return lax.ppermute(x, axes, moves)  9.12 us
    pallas_call x2, Pallas kernels, tile_device(): pl.pallas_call(functools.partial(forward_kernel, u), out_shape=[jax.Shape...  8.83 us
    pallas_call x2, Pallas kernels, tile_device(): pl.pallas_call(functools.partial(backward_kernel, u), out_shape=jax.Shape...  8.39 us
    unnamed x45, local copies, waits for them, and re-layouts  4.63 us
    pallas_call x1, Pallas kernels, tile_device(): pl.pallas_call(rotate_kernel, out_shape=(part, part), in_specs=[VM] * 4,...  4.47 us
    pallas_call x1, Pallas kernels, tile_device(): pl.pallas_call(place_kernel, out_shape=jax.ShapeDtypeStruct(orbitals.shap...  4 us
  transfers between devices with their start and end apart: 17, of which 4 were waited for; matrix products, arithmetic and copies ran while one was open for 10% of the time, Pallas kernels for 9%

profile of v2, /device:TPU:0, one launch (start us, length us, event | category | flops | bytes accessed | tf_op | source)
XLA Modules:
  0.0 96.7 jit_solution(6333412481660643188)
XLA Ops:
  0.0 2.7 %slice_select_fusion = (f32[16,8,2048]{2,1,0:T(8,128)S(1)}, f32[16,8,2048]{2,1,0:T(8,128)}) fusion(f32[16,8,4096]{2,1,0:T(8,128)} %param.14, pred[]{:T(512)S(6)} %eq.87), kind=kLoop, calls=%fused_computation.4 | loop fusion | flops 524288 | bytes 4194305 | tf_op jit(solution)/shard_map/jit(_where)/select_n | solution.py:243
  2.7 0.5 collective-permute-start
  3.2 0.1 copy.20
  3.4 0.1 copy.17
  3.5 0.1 fusion.12
  3.6 0.6 gather_fusion.1
  4.2 0.2 add_reduce_fusion.1
  4.8 0.1 eq.93
  4.9 0.3 fusion.8
  5.2 0.9 convolution_select_fusion.1.own
  6.1 0.9 convolution_select_fusion.sib
  6.9 1.0 %copy-done.4 = f32[16,8,2048]{2,1,0:T(8,128)} copy-done((f32[16,8,2048]{2,1,0:T(8,128)}, f32[16,8,2048]{2,1,0:T(8,128)S(1)}, u32[]{:S(2)}) %copy-start.4) | copy-done | bytes 1048600
  7.9 4.5 %rotate.1 = (f32[16,8,2048]{2,1,0:T(8,128)}, f32[16,8,2048]{2,1,0:T(8,128)}) custom-call(f32[256,128]{1,0:T(8,128)} %convolution_select_fusion.1.own, f32[256,128]{1,0:T(8,128)} %convolution_select_fusion.sib, f32[16,8,2048]{2,1,0:T(8,128)} %get-tuple-element.29.mine, f32[16,8,2048]{2,1,0:T(8,128)} %copy-done.4), custom_call_target="tpu_custom_call" | custom-call | tf_op jit(solution)/shard_map/rotate/pallas_call | solution.py:270
  12.4 2.5 %collective-permute-start.1 = (f32[16,8,2048]{2,1,0:T(8,128)}, f32[16,8,2048]{2,1,0:T(8,128)S(1)}, u32[]{:S(2)}, u32[]{:S(2)}) collective-permute-start(f32[16,8,2048]{2,1,0:T(8,128)} %get-tuple-element.16), channel_id=1, source_target_pairs={{0,8},{1,9},{2,10},{3,11},{4,20},{5,21},{6,22},{7,23},{8,0},{9,1},... | collective-permute-start | bytes 3145736 | tf_op jit(solution)/shard_map/ppermute | solution.py:235
  14.9 13.0 %collective-permute-done.1 = f32[16,8,2048]{2,1,0:T(8,128)S(1)} collective-permute-done((f32[16,8,2048]{2,1,0:T(8,128)}, f32[16,8,2048]{2,1,0:T(8,128)S(1)}, u32[]{:S(2)}, u32[]{:S(2)}) %collective-permute-start.1) | collective-permute-done | bytes 1048608 | tf_op jit(solution)/shard_map/ppermute | solution.py:235
  27.8 1.3 %add.228 = f32[16,8,2048]{2,1,0:T(8,128)S(1)} add(f32[16,8,2048]{2,1,0:T(8,128)} %get-tuple-element.15, f32[16,8,2048]{2,1,0:T(8,128)S(1)} %collective-permute-done.1) | non-fusion elementwise | flops 262144 | bytes 3145728 | tf_op jit(solution)/shard_map/add | solution.py:273
  29.3 2.1 %collective-permute-start.2 = (f32[8,8,2048]{2,1,0:T(8,128)S(1)}, f32[8,8,2048]{2,1,0:T(8,128)S(1)}, u32[]{:S(2)}, u32[]{:S(2)}) collective-permute-start(f32[8,8,2048]{2,1,0:T(8,128)S(1)} %slice.48), channel_id=1, source_target_pairs={{0,16},{1,17},{2,18},{3,19},{4,12},{5,13},{6,14},{7,15},{8,24},{9,... | collective-permute-start | bytes 1572872 | tf_op jit(solution)/shard_map/ppermute | solution.py:235
  31.4 7.1 %collective-permute-done.2 = f32[8,8,2048]{2,1,0:T(8,128)S(1)} collective-permute-done((f32[8,8,2048]{2,1,0:T(8,128)S(1)}, f32[8,8,2048]{2,1,0:T(8,128)S(1)}, u32[]{:S(2)}, u32[]{:S(2)}) %collective-permute-start.2) | collective-permute-done | bytes 524320 | tf_op jit(solution)/shard_map/ppermute | solution.py:235
  38.7 0.7 pad_add_fusion.1.where
  39.4 0.1 mul.188
  39.9 1.5 %fusion.7 = (f32[512,128]{1,0:T(8,128)}, f32[512,128]{1,0:T(8,128)}, f32[512,128]{1,0:T(8,128)}, f32[512,128]{1,0:T(8,128)}, f32[512,128]{1,0:T(8,128)}, /*index=5*/f32[512,128]{1,0:T(8,128)}) fusion(f32[512]{0:T(512)S(1)} %mul.188, f32[64,128]{1,0:T(8,128)S(1)} %copy-done.19, f32[512]{0:T(512)S(1)} %mul.168, f32[64,128]{1,0:T(8,128)S(1)} %copy-done.20, ...), kind=kLoop, calls=%fused_computation.20 | loop fusion | flops 655360 | bytes 1646592 | tf_op jit(solution)/shard_map/mul | solution.py:287
  41.4 0.7 copy-done.2
  42.1 4.4 %forward_1.1 = (f32[512,256]{1,0:T(8,128)}, f32[64,256]{1,0:T(8,128)}, f32[64,256]{1,0:T(8,128)}, f32[64,256]{1,0:T(8,128)}) custom-call(s32[2]{0:T(128)} %pad_add_fusion.1.where, f32[8,8,2048]{2,1,0:T(8,128)} %copy-done.1, f32[6,8,2048]{2,1,0:T(8,128)} %copy-done.2, bf16[512,512]{1,0:T(8,128)(2,1)} %constant.127.clone.y_hi, ...), custom_call_target="tpu_custom_call" | custom-call | tf_op jit(solution)/shard_map/forward_1/pallas_call | solution.py:305
  46.5 2.1 %collective-permute-start.7 = (f32[64,256]{1,0:T(8,128)}, f32[64,256]{1,0:T(8,128)S(1)}, u32[]{:S(2)}, u32[]{:S(2)}) collective-permute-start(f32[64,256]{1,0:T(8,128)} %get-tuple-element.22), channel_id=1, source_target_pairs={{0,1},{1,0},{2,3},{3,2},{4,5},{5,4},{6,7},{7,6},{8,9},{9,8},{10,11... | collective-permute-start | bytes 196616 | tf_op jit(solution)/shard_map/ppermute | solution.py:239
  48.6 0.5 fusion.15
  50.4 2.7 %collective-permute-start.8 = (f32[64,256]{1,0:T(8,128)}, f32[64,256]{1,0:T(8,128)S(1)}, u32[]{:S(2)}, u32[]{:S(2)}) collective-permute-start(f32[64,256]{1,0:T(8,128)} %get-tuple-element.23), channel_id=1, source_target_pairs={{0,2},{1,3},{2,0},{3,1},{4,6},{5,7},{6,4},{7,5},{8,10},{9,11},{10,... | collective-permute-start | bytes 196616 | tf_op jit(solution)/shard_map/ppermute | solution.py:239
  53.1 4.4 %forward_0.1 = (f32[512,256]{1,0:T(8,128)}, f32[64,256]{1,0:T(8,128)}, f32[64,256]{1,0:T(8,128)}, f32[64,256]{1,0:T(8,128)}) custom-call(s32[2]{0:T(128)} %pad_add_fusion.1.where, f32[8,8,2048]{2,1,0:T(8,128)} %copy-done.1, f32[6,8,2048]{2,1,0:T(8,128)} %copy-done.2, bf16[512,512]{1,0:T(8,128)(2,1)} %constant.127.clone.y_hi, ...), custom_call_target="tpu_custom_call" | custom-call | tf_op jit(solution)/shard_map/forward_0/pallas_call | solution.py:305
  57.5 0.9 collective-permute-start.4
  58.4 3.5 %collective-permute-start.5 = (f32[64,256]{1,0:T(8,128)}, f32[64,256]{1,0:T(8,128)S(1)}, u32[]{:S(2)}, u32[]{:S(2)}) collective-permute-start(f32[64,256]{1,0:T(8,128)} %get-tuple-element.19), channel_id=1, source_target_pairs={{0,2},{1,3},{2,0},{3,1},{4,6},{5,7},{6,4},{7,5},{8,10},{9,11},{10,... | collective-permute-start | bytes 196616 | tf_op jit(solution)/shard_map/ppermute | solution.py:239
  61.9 0.8 dynamic-slice_convert_fusion
  62.7 0.7 reshape.371.flags
  63.3 0.6 copy-done.16
  64.0 4.2 %backward_1.1 = f32[8,4096]{1,0:T(8,128)} custom-call(s32[2]{0:T(128)} %pad_add_fusion.1.where, f32[8]{0:T(128)} %reshape.371.flags, f32[8,8,2048]{2,1,0:T(8,128)} %copy-done.1, f32[6,8,2048]{2,1,0:T(8,128)} %copy-done.2, bf16[512,512]{1,0:T(8,128)(2,1)} %constant.127.clone.y_hi, bf16[512,512]{1,0:T(8,128)(2,1)} %constant.128.clone.y_lo, ...), custom_call_target="tpu_custom_call" | custom-call | tf_op jit(solution)/shard_map/backward_1/pallas_call | solution.py:318
  68.2 0.6 copy-done.14
  68.8 4.2 %backward_0.1 = f32[8,4096]{1,0:T(8,128)} custom-call(s32[2]{0:T(128)} %pad_add_fusion.1.where, f32[8]{0:T(128)} %reshape.371.flags, f32[8,8,2048]{2,1,0:T(8,128)} %copy-done.1, f32[6,8,2048]{2,1,0:T(8,128)} %copy-done.2, bf16[512,512]{1,0:T(8,128)(2,1)} %constant.127.clone.y_hi, bf16[512,512]{1,0:T(8,128)(2,1)} %constant.128.clone.y_lo, ...), custom_call_target="tpu_custom_call" | custom-call | tf_op jit(solution)/shard_map/backward_0/pallas_call | solution.py:318
  73.0 0.9 pad_maximum_fusion.refs_0_
  74.0 1.7 %collective-permute-start.10 = (f32[2,8,4096]{2,1,0:T(8,128)S(1)}, f32[2,8,4096]{2,1,0:T(8,128)S(1)}, u32[]{:S(2)}, u32[]{:S(2)}) collective-permute-start(f32[2,8,4096]{2,1,0:T(8,128)S(1)} %pad_maximum_fusion.refs_0_), channel_id=1, source_target_pairs={{0,8},{1,9},{2,10},{3,11},{4,20},{5,21},{6,22},{7,23},{8,0},{9,1},... | collective-permute-start | bytes 786440 | tf_op jit(solution)/shard_map/ppermute | solution.py:235
  75.9 1.5 %collective-permute-start.11 = (f32[2,8,4096]{2,1,0:T(8,128)S(1)}, f32[2,8,4096]{2,1,0:T(8,128)S(1)}, u32[]{:S(2)}, u32[]{:S(2)}) collective-permute-start(f32[2,8,4096]{2,1,0:T(8,128)S(1)} %pad_maximum_fusion.refs_0_), channel_id=1, source_target_pairs={{0,16},{1,17},{2,18},{3,19},{4,12},{5,13},{6,14},{7,15},{8,24},{9,... | collective-permute-start | bytes 786440 | tf_op jit(solution)/shard_map/ppermute | solution.py:235
  77.4 5.8 %collective-permute-done.10.refs_1_ = f32[2,8,4096]{2,1,0:T(8,128)S(1)} collective-permute-done((f32[2,8,4096]{2,1,0:T(8,128)S(1)}, f32[2,8,4096]{2,1,0:T(8,128)S(1)}, u32[]{:S(2)}, u32[]{:S(2)}) %collective-permute-start.10) | collective-permute-done | bytes 262176 | tf_op jit(solution)/shard_map/ppermute | solution.py:235
  83.2 0.6 collective-permute-start.12
  83.9 0.5 collective-permute-start.14
  84.5 5.1 %collective-permute-done.12.refs_3_ = f32[2,8,4096]{2,1,0:T(8,128)S(1)} collective-permute-done((f32[2,8,4096]{2,1,0:T(8,128)S(1)}, f32[2,8,4096]{2,1,0:T(8,128)S(1)}, u32[]{:S(2)}, u32[]{:S(2)}) %collective-permute-start.12) | collective-permute-done | bytes 262176 | tf_op jit(solution)/shard_map/ppermute | solution.py:235
  89.6 0.6 gather_fusion
  90.4 0.7 reshape.373.match
  91.2 0.6 copy-done.9
  91.9 0.1 copy-done.11
  92.0 0.7 copy-done.12
  92.7 4.0 %place.1 = f32[16,8,4096]{2,1,0:T(8,128)} custom-call(f32[32]{0:T(128)} %reshape.373.match, f32[2,8,4096]{2,1,0:T(8,128)} %copy-done.3, f32[2,8,4096]{2,1,0:T(8,128)} %copy-done.6, f32[2,8,4096]{2,1,0:T(8,128)} %copy-done.7, f32[2,8,4096]{2,1,0:T(8,128)} %copy-done.8, f32[2,8,4096]{2,1,0:T(8,128)} %copy-done.9, f32[2,8,4096]{2,1,0:T(8,128)} %copy-done.10, ...), custom_call_target="tpu_custom_call" | custom-call | tf_op jit(solution)/shard_map/place/pallas_call | solution.py:340
  (88 shorter events, 1.8 us)
Async XLA Ops:
  0.0 4.9 %copy-start = (f32[128,128]{1,0:T(8,128)S(1)}, f32[128,128]{1,0:T(8,128)}, u32[]{:S(2)}) copy-start(f32[128,128]{1,0:T(8,128)} %param.15) | copy-start | bytes 196612
  0.0 3.2 %copy-start.21 = (s32[4,2]{0,1:T(2,128)S(1)}, s32[4,2]{0,1:T(2,128)}, u32[]{:S(2)}) copy-start(s32[4,2]{0,1:T(2,128)} %param.16) | copy-start | bytes 100
  2.7 4.2 %collective-permute-start = (f32[16,8,2048]{2,1,0:T(8,128)S(1)}, f32[16,8,2048]{2,1,0:T(8,128)S(1)}, u32[]{:S(2)}, u32[]{:S(2)}) collective-permute-start(f32[16,8,2048]{2,1,0:T(8,128)S(1)} %get-tuple-element.28), channel_id=1, source_target_pairs={{0,4},{1,5},{2,6},{3,7},{4,0},{5,1},{6,2},{7,3},{8,12},{9,13},{10,... | collective-permute-start | bytes 3145736 | tf_op jit(solution)/shard_map/ppermute | solution.py:235
  6.9 1.0 %copy-start.4 = (f32[16,8,2048]{2,1,0:T(8,128)}, f32[16,8,2048]{2,1,0:T(8,128)S(1)}, u32[]{:S(2)}) copy-start(f32[16,8,2048]{2,1,0:T(8,128)S(1)} %collective-permute-done.theirs) | copy-start | bytes 3145732
  12.4 15.5 %collective-permute-start.1 = (f32[16,8,2048]{2,1,0:T(8,128)}, f32[16,8,2048]{2,1,0:T(8,128)S(1)}, u32[]{:S(2)}, u32[]{:S(2)}) collective-permute-start(f32[16,8,2048]{2,1,0:T(8,128)} %get-tuple-element.16), channel_id=1, source_target_pairs={{0,8},{1,9},{2,10},{3,11},{4,20},{5,21},{6,22},{7,23},{8,0},{9,1},... | collective-permute-start | bytes 3145736 | tf_op jit(solution)/shard_map/ppermute | solution.py:235
  29.2 10.7 %copy-start.19 = (f32[64,128]{1,0:T(8,128)S(1)}, f32[64,128]{1,0:T(8,128)}, u32[]{:S(2)}) copy-start(f32[64,128]{1,0:T(8,128)} %constant.123.clone) | copy-start | bytes 98308
  29.2 10.7 %copy-start.20 = (f32[64,128]{1,0:T(8,128)S(1)}, f32[64,128]{1,0:T(8,128)}, u32[]{:S(2)}) copy-start(f32[64,128]{1,0:T(8,128)} %constant.124.clone) | copy-start | bytes 98308
  29.3 9.3 %collective-permute-start.2 = (f32[8,8,2048]{2,1,0:T(8,128)S(1)}, f32[8,8,2048]{2,1,0:T(8,128)S(1)}, u32[]{:S(2)}, u32[]{:S(2)}) collective-permute-start(f32[8,8,2048]{2,1,0:T(8,128)S(1)} %slice.48), channel_id=1, source_target_pairs={{0,16},{1,17},{2,18},{3,19},{4,12},{5,13},{6,14},{7,15},{8,24},{9,... | collective-permute-start | bytes 1572872 | tf_op jit(solution)/shard_map/ppermute | solution.py:235
  38.6 2.8 %copy-start.1 = (f32[8,8,2048]{2,1,0:T(8,128)}, f32[8,8,2048]{2,1,0:T(8,128)S(1)}, u32[]{:S(2)}) copy-start(f32[8,8,2048]{2,1,0:T(8,128)S(1)} %slice_add_fusion.own) | copy-start | bytes 1572868
  38.6 2.7 %collective-permute-start.3 = (f32[6,8,2048]{2,1,0:T(8,128)S(1)}, f32[6,8,2048]{2,1,0:T(8,128)S(1)}, u32[]{:S(2)}, u32[]{:S(2)}) collective-permute-start(f32[6,8,2048]{2,1,0:T(8,128)S(1)} %slice.49), channel_id=1, source_target_pairs={{0,4},{1,5},{2,6},{3,7},{4,0},{5,1},{6,2},{7,3},{8,12},{9,13},{10,... | collective-permute-start | bytes 1179656 | tf_op jit(solution)/shard_map/ppermute | solution.py:235
  41.3 0.8 copy-start.2
  46.5 15.3 %collective-permute-start.7 = (f32[64,256]{1,0:T(8,128)}, f32[64,256]{1,0:T(8,128)S(1)}, u32[]{:S(2)}, u32[]{:S(2)}) collective-permute-start(f32[64,256]{1,0:T(8,128)} %get-tuple-element.22), channel_id=1, source_target_pairs={{0,1},{1,0},{2,3},{3,2},{4,5},{5,4},{6,7},{7,6},{8,9},{9,8},{10,11... | collective-permute-start | bytes 196616 | tf_op jit(solution)/shard_map/ppermute | solution.py:239
  50.4 12.9 %collective-permute-start.8 = (f32[64,256]{1,0:T(8,128)}, f32[64,256]{1,0:T(8,128)S(1)}, u32[]{:S(2)}, u32[]{:S(2)}) collective-permute-start(f32[64,256]{1,0:T(8,128)} %get-tuple-element.23), channel_id=1, source_target_pairs={{0,2},{1,3},{2,0},{3,1},{4,6},{5,7},{6,4},{7,5},{8,10},{9,11},{10,... | collective-permute-start | bytes 196616 | tf_op jit(solution)/shard_map/ppermute | solution.py:239
  53.1 10.3 %collective-permute-start.9 = (f32[64,256]{1,0:T(8,128)}, f32[64,256]{1,0:T(8,128)S(1)}, u32[]{:S(2)}, u32[]{:S(2)}) collective-permute-start(f32[64,256]{1,0:T(8,128)} %get-tuple-element.24), channel_id=1, source_target_pairs={{0,3},{1,2},{2,1},{3,0},{4,7},{5,6},{6,5},{7,4},{8,11},{9,10},{10,... | collective-permute-start | bytes 196616 | tf_op jit(solution)/shard_map/ppermute | solution.py:239
  57.5 10.7 %collective-permute-start.4 = (f32[64,256]{1,0:T(8,128)}, f32[64,256]{1,0:T(8,128)S(1)}, u32[]{:S(2)}, u32[]{:S(2)}) collective-permute-start(f32[64,256]{1,0:T(8,128)} %get-tuple-element.18), channel_id=1, source_target_pairs={{0,1},{1,0},{2,3},{3,2},{4,5},{5,4},{6,7},{7,6},{8,9},{9,8},{10,11... | collective-permute-start | bytes 196616 | tf_op jit(solution)/shard_map/ppermute | solution.py:239
  58.4 9.8 %collective-permute-start.5 = (f32[64,256]{1,0:T(8,128)}, f32[64,256]{1,0:T(8,128)S(1)}, u32[]{:S(2)}, u32[]{:S(2)}) collective-permute-start(f32[64,256]{1,0:T(8,128)} %get-tuple-element.19), channel_id=1, source_target_pairs={{0,2},{1,3},{2,0},{3,1},{4,6},{5,7},{6,4},{7,5},{8,10},{9,11},{10,... | collective-permute-start | bytes 196616 | tf_op jit(solution)/shard_map/ppermute | solution.py:239
  61.9 1.5 %copy-start.13 = (f32[64,256]{1,0:T(8,128)}, f32[64,256]{1,0:T(8,128)S(1)}, u32[]{:S(2)}) copy-start(f32[64,256]{1,0:T(8,128)S(1)} %collective-permute-done.7.rest_0_) | copy-start | bytes 196612
  61.9 6.3 %collective-permute-start.6 = (f32[64,256]{1,0:T(8,128)}, f32[64,256]{1,0:T(8,128)S(1)}, u32[]{:S(2)}, u32[]{:S(2)}) collective-permute-start(f32[64,256]{1,0:T(8,128)} %get-tuple-element.20), channel_id=1, source_target_pairs={{0,3},{1,2},{2,1},{3,0},{4,7},{5,6},{6,5},{7,4},{8,11},{9,10},{10,... | collective-permute-start | bytes 196616 | tf_op jit(solution)/shard_map/ppermute | solution.py:239
  63.3 0.6 copy-start.16
  63.3 0.6 copy-start.17
  68.2 4.9 %copy-start.5 = (f32[8,4096]{1,0:T(8,128)S(1)}, f32[8,4096]{1,0:T(8,128)}, u32[]{:S(2)}) copy-start(f32[8,4096]{1,0:T(8,128)} %backward_1.1) | copy-start | bytes 393220
  68.2 0.6 copy-start.14
  68.2 0.6 copy-start.15
  68.2 0.6 copy-start.18
  74.0 17.2 %copy-start.3 = (f32[2,8,4096]{2,1,0:T(8,128)}, f32[2,8,4096]{2,1,0:T(8,128)S(1)}, u32[]{:S(2)}) copy-start(f32[2,8,4096]{2,1,0:T(8,128)S(1)} %pad_maximum_fusion.refs_0_) | copy-start | bytes 786436
  74.0 9.2 %collective-permute-start.10 = (f32[2,8,4096]{2,1,0:T(8,128)S(1)}, f32[2,8,4096]{2,1,0:T(8,128)S(1)}, u32[]{:S(2)}, u32[]{:S(2)}) collective-permute-start(f32[2,8,4096]{2,1,0:T(8,128)S(1)} %pad_maximum_fusion.refs_0_), channel_id=1, source_target_pairs={{0,8},{1,9},{2,10},{3,11},{4,20},{5,21},{6,22},{7,23},{8,0},{9,1},... | collective-permute-start | bytes 786440 | tf_op jit(solution)/shard_map/ppermute | solution.py:235
  75.9 8.5 %collective-permute-start.11 = (f32[2,8,4096]{2,1,0:T(8,128)S(1)}, f32[2,8,4096]{2,1,0:T(8,128)S(1)}, u32[]{:S(2)}, u32[]{:S(2)}) collective-permute-start(f32[2,8,4096]{2,1,0:T(8,128)S(1)} %pad_maximum_fusion.refs_0_), channel_id=1, source_target_pairs={{0,16},{1,17},{2,18},{3,19},{4,12},{5,13},{6,14},{7,15},{8,24},{9,... | collective-permute-start | bytes 786440 | tf_op jit(solution)/shard_map/ppermute | solution.py:235
  83.2 7.9 %copy-start.6 = (f32[2,8,4096]{2,1,0:T(8,128)}, f32[2,8,4096]{2,1,0:T(8,128)S(1)}, u32[]{:S(2)}) copy-start(f32[2,8,4096]{2,1,0:T(8,128)S(1)} %collective-permute-done.10.refs_1_) | copy-start | bytes 786436
  83.2 6.4 %collective-permute-start.12 = (f32[2,8,4096]{2,1,0:T(8,128)S(1)}, f32[2,8,4096]{2,1,0:T(8,128)S(1)}, u32[]{:S(2)}, u32[]{:S(2)}) collective-permute-start(f32[2,8,4096]{2,1,0:T(8,128)S(1)} %collective-permute-done.10.refs_1_), channel_id=1, source_target_pairs={{0,16},{1,17},{2,18},{3,19},{4,12},{5,13},{6,14},{7,15},{8,24},{9,... | collective-permute-start | bytes 786440 | tf_op jit(solution)/shard_map/ppermute | solution.py:235
  83.8 7.3 %collective-permute-start.13 = (f32[2,8,4096]{2,1,0:T(8,128)S(1)}, f32[2,8,4096]{2,1,0:T(8,128)S(1)}, u32[]{:S(2)}, u32[]{:S(2)}) collective-permute-start(f32[2,8,4096]{2,1,0:T(8,128)S(1)} %pad_maximum_fusion.refs_0_), channel_id=1, source_target_pairs={{0,4},{1,5},{2,6},{3,7},{4,0},{5,1},{6,2},{7,3},{8,12},{9,13},{10,... | collective-permute-start | bytes 786440 | tf_op jit(solution)/shard_map/ppermute | solution.py:235
  83.9 7.2 %collective-permute-start.14 = (f32[2,8,4096]{2,1,0:T(8,128)S(1)}, f32[2,8,4096]{2,1,0:T(8,128)S(1)}, u32[]{:S(2)}, u32[]{:S(2)}) collective-permute-start(f32[2,8,4096]{2,1,0:T(8,128)S(1)} %collective-permute-done.10.refs_1_), channel_id=1, source_target_pairs={{0,4},{1,5},{2,6},{3,7},{4,0},{5,1},{6,2},{7,3},{8,12},{9,13},{10,... | collective-permute-start | bytes 786440 | tf_op jit(solution)/shard_map/ppermute | solution.py:235
  84.4 6.8 %copy-start.7 = (f32[2,8,4096]{2,1,0:T(8,128)}, f32[2,8,4096]{2,1,0:T(8,128)S(1)}, u32[]{:S(2)}) copy-start(f32[2,8,4096]{2,1,0:T(8,128)S(1)} %collective-permute-done.11.refs_2_) | copy-start | bytes 786436
  84.4 6.7 %collective-permute-start.15 = (f32[2,8,4096]{2,1,0:T(8,128)S(1)}, f32[2,8,4096]{2,1,0:T(8,128)S(1)}, u32[]{:S(2)}, u32[]{:S(2)}) collective-permute-start(f32[2,8,4096]{2,1,0:T(8,128)S(1)} %collective-permute-done.11.refs_2_), channel_id=1, source_target_pairs={{0,4},{1,5},{2,6},{3,7},{4,0},{5,1},{6,2},{7,3},{8,12},{9,13},{10,... | collective-permute-start | bytes 786440 | tf_op jit(solution)/shard_map/ppermute | solution.py:235
  89.6 1.6 %copy-start.8 = (f32[2,8,4096]{2,1,0:T(8,128)}, f32[2,8,4096]{2,1,0:T(8,128)S(1)}, u32[]{:S(2)}) copy-start(f32[2,8,4096]{2,1,0:T(8,128)S(1)} %collective-permute-done.12.refs_3_) | copy-start | bytes 786436
  89.6 1.5 %collective-permute-start.16 = (f32[2,8,4096]{2,1,0:T(8,128)S(1)}, f32[2,8,4096]{2,1,0:T(8,128)S(1)}, u32[]{:S(2)}, u32[]{:S(2)}) collective-permute-start(f32[2,8,4096]{2,1,0:T(8,128)S(1)} %collective-permute-done.12.refs_3_), channel_id=1, source_target_pairs={{0,4},{1,5},{2,6},{3,7},{4,0},{5,1},{6,2},{7,3},{8,12},{9,13},{10,... | collective-permute-start | bytes 786440 | tf_op jit(solution)/shard_map/ppermute | solution.py:235
  91.1 0.7 copy-start.9
  91.1 0.8 copy-start.10
  91.1 0.9 copy-start.11
  92.0 0.7 copy-start.12
